TPU v7x, 256 devices: a whole 4x4x8 slice. The times are simulated.
256 devices in a mesh: grp: 16 (over x_hi, z), ing: 16 (over y, x_lo, core).
Axes of the slice: x: 4 (x_hi: 2, x_lo: 2; x = x_hi * 2 + x_lo), y: 4, z: 8, core: 2. Of those that a mesh axis runs over, the one named last changes fastest.
Arguments:
- state_vector: float32 [2, 16, 16, 131072], P(None, 'grp', 'ing'), may hold values from -6 to 6
- local_gates: float32 [2, 2, 32, 32], replicated, may hold values from -0.75 to 0.75
- local_angles: float32 [10], replicated, may hold values from -1 to 1
- pair_qubits: int32 [16, 2], replicated, may hold values from 0 to 9
- pair_angles: float32 [16], replicated, may hold values from -1 to 1
- group_gates: float32 [4, 2, 4, 4], replicated, may hold values from -2 to 2
- inner_gate: float32 [2, 32, 32], replicated, may hold values from -0.75 to 0.75
Outputs:
- new_state: float32 [2, 16, 16, 131072], P(None, 'grp', 'ing')
Inputs may be any that keep to these rules, and one draw needn't show every extreme that they name: `pair_qubits`: qubit numbers; a pair may name one qubit twice.
All inputs are finite; a program needn't handle non-finite values.
Results may differ from a plain program's by a relative error of at most 0.00011.
Values sent between devices are 32-bit elements; how exact they have to be, the bound alone decides.
No kernel may reach another device: no remote copies, remote signals or barrier semaphores. Data moves between devices by JAX's collectives and lax.ppermute only.
A program may use at most 64 MiB of HBM per device.

v0:
```python
import jax
import jax.numpy as jnp
from jax import lax
from jax.sharding import PartitionSpec as P

HIGHEST_PRECISION = lax.Precision.HIGHEST


def from_partner(value, axis, stride):
    mask = 2**stride
    pairs = [(source, source ^ mask) for source in range(lax.axis_size(axis))]
    return lax.ppermute(value, axis, pairs)


def complex_apply(matrix, shaped, pattern):
    real_part = jnp.einsum(pattern, matrix[0], shaped[0], precision=HIGHEST_PRECISION) - jnp.einsum(
        pattern, matrix[1], shaped[1], precision=HIGHEST_PRECISION
    )
    imag_part = jnp.einsum(pattern, matrix[0], shaped[1], precision=HIGHEST_PRECISION) + jnp.einsum(
        pattern, matrix[1], shaped[0], precision=HIGHEST_PRECISION
    )
    return jnp.stack([real_part, imag_part])


def block_gate(flat, matrix, start):
    length = flat.shape[1]
    shaped = flat.reshape(2, length >> start + 5, 32, 1 << start)
    return complex_apply(matrix, shaped, "ab,hbl->hal").reshape(2, length)


def single_gate(flat, matrix, qubit):
    length = flat.shape[1]
    shaped = flat.reshape(2, length >> qubit + 1, 2, 1 << qubit)
    return complex_apply(matrix, shaped, "xy,hyl->hxl").reshape(2, length)


def phase_angles(length, local_angles, pair_qubits, pair_angles):
    position = lax.iota(jnp.int32, length)
    phases = jnp.zeros((length,), jnp.float32)
    for qubit in range(local_angles.shape[0]):
        sign_value = (1 - 2 * (position >> qubit & 1)).astype(jnp.float32)
        phases = phases + local_angles[qubit] * sign_value
    for entry in range(pair_qubits.shape[0]):
        sign_first = 1 - 2 * (position >> pair_qubits[entry, 0] & 1)
        sign_second = 1 - 2 * (position >> pair_qubits[entry, 1] & 1)
        phases = phases + pair_angles[entry] * (sign_first * sign_second).astype(jnp.float32)
    return phases


def apply_phase(shaped, phases):
    cosine = jnp.cos(phases)
    sine = jnp.sin(phases)
    return jnp.stack([cosine * shaped[0] - sine * shaped[1], sine * shaped[0] + cosine * shaped[1]])


def on_device(
    state_vector, local_gates, local_angles, pair_qubits, pair_angles, group_gates, inner_gate
):
    length = state_vector.shape[-1]
    local_bits = length.bit_length() - 1
    group_count = lax.axis_size("grp")
    inner_count = lax.axis_size("ing")
    group_bits = group_count.bit_length() - 1
    flat = state_vector.reshape(2, length)
    flat = block_gate(flat, local_gates[0], local_bits - 5)
    flat = block_gate(flat, local_gates[1], local_bits - 10)
    phases = phase_angles(length, local_angles, pair_qubits, pair_angles)
    flat = apply_phase(flat.reshape(2, 1, length), phases).reshape(2, length)
    group_index = lax.axis_index("grp")
    for level in range(group_bits):
        partner = from_partner(flat, "grp", level)
        own_bit = group_index >> level & 1
        matrix = group_gates[level].reshape(2, 2, 2, 2, 2)
        rows = lax.dynamic_index_in_dim(matrix, own_bit, 1, keepdims=False)
        own_part = lax.dynamic_index_in_dim(rows, own_bit, 2, keepdims=False)
        cross_part = lax.dynamic_index_in_dim(rows, 1 - own_bit, 2, keepdims=False)
        low_qubit = local_bits - 10 + level
        flat = single_gate(flat, own_part, low_qubit) + single_gate(partner, cross_part, low_qubit)
    top_count = 32 // inner_count
    sectioned_inner = flat.reshape(2, top_count, inner_count, length // 32)
    permuted_gate = (
        inner_gate.reshape(2, inner_count, top_count, inner_count, top_count)
        .transpose(0, 2, 1, 4, 3)
        .reshape(2, 32, 32)
    )
    received = lax.all_to_all(sectioned_inner, "ing", split_axis=2, concat_axis=2, tiled=True)
    shaped = received.reshape(2, 1, 32, -1)
    working = complex_apply(permuted_gate, shaped, "ab,hbl->hal").reshape(received.shape)
    flat = lax.all_to_all(working, "ing", split_axis=2, concat_axis=2, tiled=True)
    return flat.reshape(state_vector.shape)


def solution(mesh):
    return jax.shard_map(
        on_device,
        mesh=mesh,
        in_specs=(P(None, "grp", "ing", None), P(), P(), P(), P(), P(), P()),
        out_specs=P(None, "grp", "ing", None),
        check_vma=False,
    )
```

profile of v0, /device:TPU:1, one launch (start us, length us, event | category | flops | bytes accessed | tf_op | source)
XLA Modules:
  0.0 433.9 jit_solution(7098205976518890446)
XLA Ops:
  0.0 2.1 fusion.42
  4.2 43.2 %fusion.37 = (f32[32,32,128]{2,1,0:T(8,128)S(1)}, f32[32,32,128]{2,1,0:T(8,128)}) fusion(s32[]{:T(128)} %bitcast.57, s32[]{:T(128)} %bitcast.56, f32[]{:T(128)} %bitcast.55, s32[]{:T(128)} %bitcast.54, s32[]{:T(128)} %bitcast.53, f32[]{:T(128)} %bitcast.52, s32[]{:T(128)} %bitcast.51, s32[]{:T(128)} %bitcast.50, f32[]{:T(128)} %bitcast.49, s32[]{:T(128)} %bitcast.48, ...), kind=kLoop, calls=%fused_computation.104 | loop fusion | flops 34734080 | bytes 1048808 | tf_op jit(solution)/shard_map/sin | solution.py:52
  47.4 91.6 %fusion.36 = (f32[1,1,131072]{2,1,0:T(1,128)S(1)}, f32[1,1,131072]{2,1,0:T(1,128)S(1)}) fusion(s32[]{:T(128)} %bitcast.57, s32[]{:T(128)} %bitcast.56, f32[]{:T(128)} %bitcast.55, s32[]{:T(128)} %bitcast.54, s32[]{:T(128)} %bitcast.53, f32[]{:T(128)} %bitcast.52, s32[]{:T(128)} %bitcast.51, s32[]{:T(128)} %bitcast.50, f32[]{:T(128)} %bitcast.49, ...), kind=kLoop, calls=%fused_computation.103 | loop fusion | flops 34209792 | bytes 1048808 | tf_op jit(solution)/shard_map/sin | solution.py:52
  139.0 2.7 slice_reduce_fusion.13
  147.4 2.2 fusion.14
  149.6 14.4 %multiply_subtract_fusion = (f32[1,1,131072]{2,1,0:T(1,128)S(1)}, f32[1,1,131072]{2,1,0:T(1,128)S(1)}) fusion(f32[1,1,131072]{2,1,0:T(1,128)S(1)} %get-tuple-element.19, f32[1,1,131072]{2,1,0:T(1,128)S(1)} %bitcast.322, f32[1,1,131072]{2,1,0:T(1,128)S(1)} %bitcast.310, f32[1,1,131072]{2,1,0:T(1,128)S(1)} %get-tuple-element.20), kind=kLoop, calls=%fused_computation.62 | loop fusion | flops 786432 | bytes 3145728 | tf_op jit(solution)/shard_map/sub | solution.py:53
  165.8 2.7 collective-permute-start
  171.5 1.9 fusion.47
  173.4 1.9 convolution_subtract_fusion.9
  175.4 1.9 convolution_add_fusion.9
  177.3 13.0 %collective-permute-done = f32[2,131072]{1,0:T(2,128)S(1)} collective-permute-done((f32[2,131072]{1,0:T(2,128)S(1)}, f32[2,131072]{1,0:T(2,128)S(1)}, u32[]{:S(2)}, u32[]{:S(2)}) %collective-permute-start) | collective-permute-done | bytes 1048608 | tf_op jit(solution)/shard_map/ppermute | solution.py:12
  193.0 2.1 fusion.49
  195.2 1.9 convolution_subtract_fusion.8
  197.1 1.9 convolution_add_fusion.8
  200.8 6.0 %collective-permute-start.1 = (f32[2,131072]{1,0:T(2,128)S(1)}, f32[2,131072]{1,0:T(2,128)}, u32[]{:S(2)}, u32[]{:S(2)}) collective-permute-start(f32[2,131072]{1,0:T(2,128)S(1)} %maximum_add_fusion), channel_id=1, source_target_pairs={{0,32},{16,48},{32,0},{48,16},{64,96},{80,112},{96,64},{112,80},{1... | collective-permute-start | bytes 3145736 | tf_op jit(solution)/shard_map/ppermute | solution.py:12
  206.8 2.7 slice_reduce_fusion.11
  210.2 1.9 fusion.50
  212.1 1.9 fusion.11
  216.8 2.1 fusion.10
  219.7 32.2 %collective-permute-done.1 = f32[2,131072]{1,0:T(2,128)} collective-permute-done((f32[2,131072]{1,0:T(2,128)S(1)}, f32[2,131072]{1,0:T(2,128)}, u32[]{:S(2)}, u32[]{:S(2)}) %collective-permute-start.1) | collective-permute-done | bytes 1048608 | tf_op jit(solution)/shard_map/ppermute | solution.py:12
  251.9 4.4 %slice_reduce_fusion.8 = (f32[131072]{0:T(1024)S(1)}, f32[131072]{0:T(1024)S(1)}) fusion(f32[2,131072]{1,0:T(2,128)} %collective-permute-done.1), kind=kLoop, calls=%fused_computation.51 | loop fusion | bytes 2097152 | tf_op jit(solution)/shard_map/slice | solution.py:17
  260.8 2.7 fusion.9
  265.4 2.4 fusion.8
  270.3 6.5 %collective-permute-start.2 = (f32[2,131072]{1,0:T(2,128)S(1)}, f32[2,131072]{1,0:T(2,128)}, u32[]{:S(2)}, u32[]{:S(2)}) collective-permute-start(f32[2,131072]{1,0:T(2,128)S(1)} %maximum_add_fusion.1), channel_id=1, source_target_pairs={{0,64},{16,80},{32,96},{48,112},{64,0},{80,16},{96,32},{112,48},{1... | collective-permute-start | bytes 3145736 | tf_op jit(solution)/shard_map/ppermute | solution.py:12
  276.8 2.7 slice_reduce_fusion.7
  282.0 1.9 fusion.7
  286.7 2.1 fusion.6
  289.6 32.5 %collective-permute-done.2 = f32[2,131072]{1,0:T(2,128)} collective-permute-done((f32[2,131072]{1,0:T(2,128)S(1)}, f32[2,131072]{1,0:T(2,128)}, u32[]{:S(2)}, u32[]{:S(2)}) %collective-permute-start.2) | collective-permute-done | bytes 1048608 | tf_op jit(solution)/shard_map/ppermute | solution.py:12
  322.2 4.4 %slice_reduce_fusion.4 = (f32[131072]{0:T(1024)S(1)}, f32[131072]{0:T(1024)S(1)}) fusion(f32[2,131072]{1,0:T(2,128)} %collective-permute-done.2), kind=kLoop, calls=%fused_computation.47 | loop fusion | bytes 2097152 | tf_op jit(solution)/shard_map/slice | solution.py:17
  329.0 1.9 fusion.57
  330.9 2.7 fusion.5
  335.5 2.4 fusion.4
  340.5 2.9 collective-permute-start.3
  343.3 2.7 slice_reduce_fusion.3
  346.6 1.9 fusion.58
  348.5 1.9 fusion.3
  351.4 1.9 fusion.59
  353.3 2.1 fusion.2
  356.3 8.9 %collective-permute-done.3 = f32[2,131072]{1,0:T(2,128)} collective-permute-done((f32[2,131072]{1,0:T(2,128)S(1)}, f32[2,131072]{1,0:T(2,128)}, u32[]{:S(2)}, u32[]{:S(2)}) %collective-permute-start.3) | collective-permute-done | bytes 1048608 | tf_op jit(solution)/shard_map/ppermute | solution.py:12
  365.1 4.4 %slice_reduce_fusion = (f32[131072]{0:T(1024)S(1)}, f32[131072]{0:T(1024)S(1)}) fusion(f32[2,131072]{1,0:T(2,128)} %collective-permute-done.3), kind=kLoop, calls=%fused_computation.43 | loop fusion | bytes 2097152 | tf_op jit(solution)/shard_map/slice | solution.py:17
  370.1 1.9 fusion.60
  372.0 1.9 fusion.61
  373.9 2.7 fusion.1
  378.6 2.2 fusion
  383.5 8.1 %all-to-all-start = ((f32[2,2,16,4096]{3,1,0,2:T(2,128)}), f32[2,2,16,4096]{3,1,0,2:T(2,128)S(1)}, u32[]{:S(2)}, u32[]{:S(2)}) async-start(f32[2,2,16,4096]{3,1,0,2:T(2,128)} %maximum_add_fusion.3), calls=%async_computation | async-start | bytes 2097152 | tf_op jit(solution)/shard_map/all_to_all | solution.py:86
  392.7 14.8 %all-to-all-done = f32[2,2,16,4096]{3,1,0,2:T(2,128)S(1)} async-done(((f32[2,2,16,4096]{3,1,0,2:T(2,128)}), f32[2,2,16,4096]{3,1,0,2:T(2,128)S(1)}, u32[]{:S(2)}, u32[]{:S(2)}) %all-to-all-start) | async-done | bytes 1048608 | tf_op jit(solution)/shard_map/all_to_all | solution.py:86
  412.1 18.8 %all_to_all.10 = f32[2,2,16,4096]{3,1,0,2:T(2,128)S(1)} all-to-all(f32[2,2,16,4096]{3,1,0,2:T(2,128)S(1)} %pad_maximum_fusion.1), channel_id=1, replica_groups=mesh['grp'=16,'ing'=16] {'ing'}, dimensions={2} | all-to-all | bytes 2097152 | tf_op jit(solution)/shard_map/all_to_all | solution.py:89
  431.6 2.1 reshape.1240
  (97 shorter events, 56.2 us)
Async XLA Ops:
  0.0 2.1 copy-start.3
  2.1 0.7 copy-start.4
  2.8 0.7 copy-start.5
  4.2 134.8 %copy-start.1 = (f32[2,1,1,131072]{3,2,1,0:T(1,128)S(1)}, f32[2,1,1,131072]{3,2,1,0:T(1,128)}, u32[]{:S(2)}) copy-start(f32[2,1,1,131072]{3,2,1,0:T(1,128)} %param.7) | copy-start | bytes 3145732
  141.8 0.8 copy-start.2
  146.3 1.0 copy-start
  165.8 24.5 %collective-permute-start = (f32[2,131072]{1,0:T(2,128)S(1)}, f32[2,131072]{1,0:T(2,128)S(1)}, u32[]{:S(2)}, u32[]{:S(2)}) collective-permute-start(f32[2,131072]{1,0:T(2,128)S(1)} %bitcast.323), channel_id=1, source_target_pairs={{0,16},{16,0},{32,48},{48,32},{64,80},{80,64},{96,112},{112,96},{1... | collective-permute-start | bytes 3145736 | tf_op jit(solution)/shard_map/ppermute | solution.py:12
  168.5 0.7 copy-start.7
  200.8 51.1 %collective-permute-start.1 = (f32[2,131072]{1,0:T(2,128)S(1)}, f32[2,131072]{1,0:T(2,128)}, u32[]{:S(2)}, u32[]{:S(2)}) collective-permute-start(f32[2,131072]{1,0:T(2,128)S(1)} %maximum_add_fusion), channel_id=1, source_target_pairs={{0,32},{16,48},{32,0},{48,16},{64,96},{80,112},{96,64},{112,80},{1... | collective-permute-start | bytes 3145736 | tf_op jit(solution)/shard_map/ppermute | solution.py:12
  270.3 51.9 %collective-permute-start.2 = (f32[2,131072]{1,0:T(2,128)S(1)}, f32[2,131072]{1,0:T(2,128)}, u32[]{:S(2)}, u32[]{:S(2)}) collective-permute-start(f32[2,131072]{1,0:T(2,128)S(1)} %maximum_add_fusion.1), channel_id=1, source_target_pairs={{0,64},{16,80},{32,96},{48,112},{64,0},{80,16},{96,32},{112,48},{1... | collective-permute-start | bytes 3145736 | tf_op jit(solution)/shard_map/ppermute | solution.py:12
  340.5 24.7 %collective-permute-start.3 = (f32[2,131072]{1,0:T(2,128)S(1)}, f32[2,131072]{1,0:T(2,128)}, u32[]{:S(2)}, u32[]{:S(2)}) collective-permute-start(f32[2,131072]{1,0:T(2,128)S(1)} %maximum_add_fusion.2), channel_id=1, source_target_pairs={{0,128},{16,144},{32,160},{48,176},{64,192},{80,208},{96,224},{112... | collective-permute-start | bytes 3145736 | tf_op jit(solution)/shard_map/ppermute | solution.py:12
  383.5 8.2 %copy-start.6 = (f32[2,32,32]{2,1,0:T(8,128)S(1)}, f32[2,32,32]{2,1,0:T(8,128)}, u32[]{:S(2)}) copy-start(f32[2,32,32]{2,1,0:T(8,128)} %param.13) | copy-start | bytes 24580
  383.5 24.0 %all-to-all-start = ((f32[2,2,16,4096]{3,1,0,2:T(2,128)}), f32[2,2,16,4096]{3,1,0,2:T(2,128)S(1)}, u32[]{:S(2)}, u32[]{:S(2)}) async-start(f32[2,2,16,4096]{3,1,0,2:T(2,128)} %maximum_add_fusion.3), calls=%async_computation | async-start | bytes 2097152 | tf_op jit(solution)/shard_map/all_to_all | solution.py:86
where the time goes:
time: 440 us; the launch traced here: 434 us
  other arithmetic  158 us (36%)
  waiting for transfers between devices  101 us (23%)
  matrix products  74.2 us (17%)
  local copies, waits for them, and re-layouts  54.3 us (12%)
  starting transfers between devices  26.2 us (6%)
  blocking collectives  18.8 us (4%)
    sin x2, other arithmetic, apply_phase(): sine = jnp.sin(phases)  135 us
    ppermute x4, waiting for transfers between devices, from_partner(): return lax.ppermute(value, axis, pairs)  86.6 us
    dot_general x11, matrix products, complex_apply(): jnp.einsum(pattern, matrix[1], shaped[0], precision=HIGHEST_PRECISION)  19.5 us
    dot_general x11, matrix products, complex_apply(): jnp.einsum(pattern, matrix[0], shaped[0], precision=HIGHEST_PRECISION)  19.5 us
    all_to_all x1, blocking collectives, on_device(): lax.all_to_all(working, 'ing', split_axis=2, concat_axis=2, tiled=True)  18.8 us
    dot_general x11, matrix products, complex_apply(): jnp.einsum(pattern, matrix[0], shaped[1], precision=HIGHEST_PRECISION)  18.1 us
    ppermute x4, starting transfers between devices, from_partner(): return lax.ppermute(value, axis, pairs)  18.1 us
    dot_general x11, matrix products, complex_apply(): jnp.einsum(pattern, matrix[1], shaped[1], precision=HIGHEST_PRECISION)  17.1 us
  transfers between devices with their start and end apart: 5, of which 5 were waited for; matrix products, arithmetic and copies ran while one was open for 11% of the time, Pallas kernels for 0%

commit v1 on v0

v1 whole, which is shorter than its diff:
```python
import jax
import jax.numpy as jnp
from jax import lax
from jax.experimental import pallas as pl
from jax.experimental.pallas import tpu as pltpu
from jax.sharding import PartitionSpec as P

F32 = jnp.float32
BF16 = jnp.bfloat16


def split(value):
    high = value.astype(BF16)
    return high, (value - high.astype(F32)).astype(BF16)


def dot(left, right, dims=((1,), (0,))):
    return lax.dot_general(left, right, (dims, ((), ())), preferred_element_type=F32)


def dot3(left, right, dims=((1,), (0,))):
    (left_high, left_low), (right_high, right_low) = left, right
    return (
        dot(left_high, right_high, dims)
        + dot(left_low, right_high, dims)
        + dot(left_high, right_low, dims)
    )


def prep_kernel(pair_ref, inner_ref, w_high, w_low, m_high, m_low):
    row = lax.broadcasted_iota(jnp.int32, (256, 8), 0)
    col = lax.broadcasted_iota(jnp.int32, (256, 8), 1)
    r_full = lax.broadcasted_iota(jnp.int32, (256, 256), 0)
    c_full = lax.broadcasted_iota(jnp.int32, (256, 256), 1)
    differ = jnp.bitwise_xor(r_full, c_full)
    for level in range(4):
        key = ((row >> 6) & 1) * 4 + (row >> 7) * 2 + ((row >> level) & 1)
        pick = (key == col).astype(F32).astype(BF16)
        keep = jnp.bitwise_and(differ, 63 - (1 << level)) == 0
        for part, out in zip(split(pair_ref[level]), (w_high, w_low)):
            half = dot(pick, part).astype(BF16)
            out[level] = jnp.where(keep, dot(half, pick, ((1,), (1,))), 0.0).astype(BF16)
    row = lax.broadcasted_iota(jnp.int32, (128, 32), 0)
    col = lax.broadcasted_iota(jnp.int32, (128, 32), 1)
    pick = ((row >> 2) == col).astype(F32).astype(BF16)
    keep = jnp.bitwise_and(differ[:128, :128], 3) == 0
    for c in range(2):
        for part, out in zip(split(inner_ref[c]), (m_high, m_low)):
            half = dot(pick, part).astype(BF16)
            out[c * 128 : c * 128 + 128] = jnp.where(keep, dot(half, pick, ((1,), (1,))), 0.0).astype(BF16)


def pre_kernel(angle_ref, qubit_ref, pair_ref, x_ref, gate_ref, out_ref, y_ref):
    real, imag = gate_ref[0, 0], gate_ref[0, 1]
    first = split(jnp.concatenate([jnp.concatenate([real, -imag], 1), jnp.concatenate([imag, real], 1)], 0))
    for start in range(0, 32, 8):
        columns = [x_ref[pl.ds(start + b, 64, stride=32), :] for b in range(8)]
        result = dot3(first, split(jnp.concatenate(columns, 1)))
        for b in range(8):
            y_ref[pl.ds(start + b, 64, stride=32), :] = result[:, b * 128 : b * 128 + 128]
    position = lax.broadcasted_iota(jnp.int32, (8, 128), 0) * 128 + lax.broadcasted_iota(jnp.int32, (8, 128), 1)
    phases = jnp.zeros((8, 128), F32)
    for qubit in range(10):
        phases = phases + angle_ref[qubit] * (1 - 2 * ((position >> qubit) & 1)).astype(F32)
    for entry in range(16):
        first_bit = lax.shift_right_logical(position, jnp.full((8, 128), qubit_ref[entry, 0], jnp.int32))
        second_bit = lax.shift_right_logical(position, jnp.full((8, 128), qubit_ref[entry, 1], jnp.int32))
        odd = jnp.bitwise_and(jnp.bitwise_xor(first_bit, second_bit), 1)
        phases = phases + pair_ref[entry] * (1 - 2 * odd).astype(F32)
    low = lax.broadcasted_iota(jnp.int32, (8, 128), 0)
    lane = lax.broadcasted_iota(jnp.int32, (8, 128), 1)
    spread = (low == jnp.bitwise_and(lane, 7)).astype(F32)
    signed = jnp.where(lane < 64, -spread, spread)

    def table(value, select):
        high, rest = split(value)
        select = select.astype(BF16)
        low_part = rest
        return dot(high, select, ((0,), (0,))) + dot(low_part, select, ((0,), (0,)))

    cosine = table(jnp.cos(phases), spread)
    sine = table(jnp.sin(phases), signed)
    real, imag = gate_ref[1, 0], gate_ref[1, 1]
    zero = jnp.zeros_like(real)
    rows = [
        [real, zero, -imag, zero],
        [zero, real, zero, -imag],
        [imag, zero, real, zero],
        [zero, imag, zero, real],
    ]
    second = jnp.concatenate([jnp.concatenate(r, 1) for r in rows], 0)
    second = split(second.T)
    sub = lax.broadcasted_iota(jnp.int32, (16, 8, 128), 1)
    for ah in range(8):
        halves = []
        for top in range(2):
            at = (top * 8 + ah) * 64
            x = jnp.concatenate([y_ref[at : at + 64], y_ref[1024 + at : 1024 + at + 64]], 0)
            z = dot3(split(x.T), second)
            z = cosine * z + sine * pltpu.roll(z, 64, 1)
            halves.append(z.reshape(16, 8, 128))
        z0, z1 = halves
        out_ref[ah, :, 0] = jnp.where(sub < 4, z0, pltpu.roll(z1, 4, 1))
        out_ref[ah, :, 1] = jnp.where(sub < 4, pltpu.roll(z0, 4, 1), z1)


def mid_kernel(x_ref, w_high, w_low, m_high, m_low, out_ref):
    inner = (m_high[...], m_low[...])
    lane = lax.broadcasted_iota(jnp.int32, (128, 128), 1)
    parts = []
    for g in range(16):
        u = dot3(inner, split(x_ref[g * 16 : g * 16 + 16].reshape(128, 128)))
        turned = pltpu.roll(u[128:], 64, 1)
        parts.append(u[:128] + jnp.where(lane < 64, -turned, turned))
    for level in range(4):
        weight = (w_high[level], w_low[level])
        new = [None] * 16
        for g in range(16):
            if g >> level & 1:
                continue
            h = g | 1 << level
            y = dot3(split(jnp.concatenate([parts[g], parts[h]], 1)), weight)
            new[g], new[h] = y[:, :128], y[:, 128:]
        parts = new
    for g in range(16):
        out_ref[g * 16 : g * 16 + 16] = parts[g].reshape(16, 8, 128)


def post_kernel(x_ref, out_ref):
    sub = lax.broadcasted_iota(jnp.int32, (16, 8, 128), 1)
    for ah in range(8):
        even, odd = x_ref[ah, :, 0], x_ref[ah, :, 1]
        z0 = jnp.where(sub < 4, even, pltpu.roll(odd, 4, 1)).reshape(128, 128)
        z1 = jnp.where(sub < 4, pltpu.roll(even, 4, 1), odd).reshape(128, 128)
        for top, z in enumerate((z0, z1)):
            at = (top * 8 + ah) * 64
            turned = z.T
            out_ref[at : at + 64] = turned[:64]
            out_ref[1024 + at : 1024 + at + 64] = turned[64:]


SMEM = pl.BlockSpec(memory_space=pltpu.SMEM)
VMEM = pl.BlockSpec(memory_space=pltpu.VMEM)
PARAMS = pltpu.CompilerParams(vmem_limit_bytes=48 << 20)


def on_device(state_vector, local_gates, local_angles, pair_qubits, pair_angles, group_gates, inner_gate):
    turned = group_gates.transpose(0, 1, 3, 2)
    real, imag = turned[:, 0], turned[:, 1]
    pairs = jnp.concatenate([jnp.concatenate([real, imag], 2), jnp.concatenate([-imag, real], 2)], 1)
    weights = pl.pallas_call(
        prep_kernel,
        out_shape=(
            jax.ShapeDtypeStruct((4, 256, 256), BF16),
            jax.ShapeDtypeStruct((4, 256, 256), BF16),
            jax.ShapeDtypeStruct((256, 128), BF16),
            jax.ShapeDtypeStruct((256, 128), BF16),
        ),
        in_specs=[VMEM, VMEM],
        out_specs=(VMEM,) * 4,
        compiler_params=PARAMS,
        name="prep",
    )(pairs, inner_gate)
    sent = pl.pallas_call(
        pre_kernel,
        out_shape=jax.ShapeDtypeStruct((8, 16, 2, 8, 128), F32),
        in_specs=[SMEM, SMEM, SMEM, VMEM, VMEM],
        out_specs=VMEM,
        scratch_shapes=[pltpu.VMEM((2048, 128), F32)],
        compiler_params=PARAMS,
        name="pre",
    )(local_angles, pair_qubits, pair_angles, state_vector.reshape(2048, 128), local_gates)
    held = lax.all_to_all(sent.reshape(256, 8, 128), ("grp", "ing"), 0, 0, tiled=True)
    done = pl.pallas_call(
        mid_kernel,
        out_shape=jax.ShapeDtypeStruct((256, 8, 128), F32),
        in_specs=[VMEM] * 5,
        out_specs=VMEM,
        compiler_params=PARAMS,
        name="mid",
    )(held, *weights)
    back = lax.all_to_all(done, ("grp", "ing"), 0, 0, tiled=True)
    out = pl.pallas_call(
        post_kernel,
        out_shape=jax.ShapeDtypeStruct((2048, 128), F32),
        in_specs=[VMEM],
        out_specs=VMEM,
        compiler_params=PARAMS,
        name="post",
    )(back.reshape(8, 16, 2, 8, 128))
    return out.reshape(state_vector.shape)


def solution(mesh):
    return jax.shard_map(
        on_device,
        mesh=mesh,
        in_specs=(P(None, "grp", "ing", None), P(), P(), P(), P(), P(), P()),
        out_specs=P(None, "grp", "ing", None),
        check_vma=False,
    )
```

time: 440 us -> 95.6 us (0.22); the launches traced: 434 us -> 95.3 us
  other arithmetic: 158 us -> 0.08 us
  matrix products: 74.2 us -> 0 us
  waiting for transfers between devices: 101 us -> 28.5 us
  local copies, waits for them, and re-layouts: 54.3 us -> 4.39 us
  blocking collectives: 18.8 us -> 37.4 us
  starting transfers between devices: 26.2 us -> 15.7 us
  Pallas kernels: 0 us -> 9.2 us
    sin x2 -> x0, other arithmetic: 135 us -> none  [apply_phase(): sine = jnp.sin(phases)]
    ppermute x4 -> x0, waiting for transfers between devices: 86.6 us -> none  [from_partner(): return lax.ppermute(value, axis, pairs)]
    dot_general x44 -> x0, matrix products: 74.2 us -> none  [the longest x11 19.5 us: complex_apply(): jnp.einsum(pattern, matrix[1], shaped[0], precision=HIGHEST_PRECISION)]
    slice x19 -> x3, local copies, waits for them, and re-layouts: 29.8 us -> 0.23 us  [on_device(): real, imag = (turned[:, 0], turned[:, 1])]
    all_to_all x1, blocking collectives: 18.8 us -> 37.4 us  [on_device(): back = lax.all_to_all(done, ('grp', 'ing'), 0, 0, tiled=True)]
    ppermute x4 -> x0, starting transfers between devices: 18.1 us -> none  [from_partner(): return lax.ppermute(value, axis, pairs)]
    sub x1 -> x0, other arithmetic: 14.4 us -> none  [apply_phase(): cosine * shaped[0] - sine * shaped[1]]
    another operation x24 -> x0, local copies, waits for them, and re-layouts: 14.3 us -> none  [the longest x18 13.7 us: complex_apply(): return jnp.stack([real_part, imag_part])]
  transfers between devices with their start and end apart: 5 -> 1, of which waited for: 5 -> 1; matrix products, arithmetic and copies ran while one was open for 11% -> 0% of each run, Pallas kernels for 0% -> 1%
where the time goes in v1:
time: 95.6 us; the launch traced here: 95.3 us
  blocking collectives  37.4 us (39%)
  waiting for transfers between devices  28.5 us (30%)
  starting transfers between devices  15.7 us (16%)
  Pallas kernels  9.2 us (10%)
  local copies, waits for them, and re-layouts  4.39 us (5%)
    all_to_all x1, blocking collectives, on_device(): back = lax.all_to_all(done, ('grp', 'ing'), 0, 0, tiled=True)  37.4 us
    all_to_all x1, waiting for transfers between devices, on_device(): lax.all_to_all(sent.reshape(256, 8, 128), ('grp', 'ing'), 0, 0, tiled=True)  28.5 us
    all_to_all x1, starting transfers between devices, on_device(): lax.all_to_all(sent.reshape(256, 8, 128), ('grp', 'ing'), 0, 0, tiled=True)  15.7 us
    unnamed x13, local copies, waits for them, and re-layouts  4.16 us
    pallas_call x1, Pallas kernels, on_device(): pl.pallas_call(pre_kernel, out_shape=jax.ShapeDtypeStruct((8, 16, 2, 8, 1...  3.93 us
    pallas_call x1, Pallas kernels, on_device(): pl.pallas_call(mid_kernel, out_shape=jax.ShapeDtypeStruct((256, 8, 128),...  2.64 us
  transfers between devices with their start and end apart: 1, of which 1 were waited for; matrix products, arithmetic and copies ran while one was open for 0% of the time, Pallas kernels for 1%

profile of v1, /device:TPU:1, one launch (start us, length us, event | category | flops | bytes accessed | tf_op | source)
XLA Modules:
  0.0 95.3 jit_solution(10631166796718904971)
XLA Ops:
  0.0 0.8 copy.8.qubit_ref
  0.8 0.0 copy-start.3
  0.8 0.0 copy-start.4
  0.8 0.7 copy-done.3
  1.4 0.0 copy-done.4
  1.4 0.0 copy-start
  1.4 1.2 %copy-done = f32[2,1,1,131072]{3,2,1,0:T(1,128)S(1)} copy-done((f32[2,1,1,131072]{3,2,1,0:T(1,128)S(1)}, f32[2,1,1,131072]{3,2,1,0:T(1,128)}, u32[]{:S(2)}) %copy-start) | copy-done | bytes 1048600
  2.7 0.0 copy-start.1
  2.7 0.8 copy-done.1
  3.5 3.9 %pre.1 = f32[8,16,2,8,128]{4,3,2,1,0:T(8,128)} custom-call(f32[10]{0:T(128)S(1)} %copy-done.3, s32[16,2]{1,0:T(8,128)S(1)} %copy.8.qubit_ref, f32[16]{0:T(128)S(1)} %copy-done.4, f32[2048,128]{1,0:T(8,128)S(1)} %bitcast.9, f32[2,2,32,32]{3,2,1,0:T(8,128)S(1)} %copy-done.1), custom_call_target="tpu_custom_call" | custom-call | tf_op jit(solution)/shard_map/pre/pallas_call | solution.py:164
  7.4 0.0 copy-start.5
  7.4 15.7 %all-to-all-start = ((f32[256,8,128]{2,1,0:T(8,128)}), f32[256,8,128]{2,1,0:T(8,128)S(1)}, u32[]{:S(2)}, u32[]{:S(2)}) async-start(f32[256,8,128]{2,1,0:T(8,128)} %bitcast.1), calls=%async_computation | async-start | bytes 2097152 | tf_op jit(solution)/shard_map/all_to_all | solution.py:173
  23.1 0.0 copy-done.5
  23.1 0.1 copy.10
  23.2 0.1 copy.9
  23.3 0.0 copy-start.2
  23.3 0.1 maximum_maximum_fusion.pair_ref
  23.4 0.7 copy-done.2
  24.1 1.3 %prep.1 = (bf16[4,256,256]{2,1,0:T(8,128)(2,1)S(1)}, bf16[4,256,256]{2,1,0:T(8,128)(2,1)S(1)}, bf16[256,128]{1,0:T(8,128)(2,1)S(1)}, bf16[256,128]{1,0:T(8,128)(2,1)S(1)}) custom-call(f32[4,8,8]{2,1,0:T(8,128)S(1)} %maximum_maximum_fusion.pair_ref, f32[2,32,32]{2,1,0:T(8,128)S(1)} %copy-done.2), custom_call_target="tpu_custom_call" | custom-call | tf_op jit(solution)/shard_map/prep/pallas_call | solution.py:151
  25.4 28.5 %all-to-all-done.x_ref = f32[256,8,128]{2,1,0:T(8,128)S(1)} async-done(((f32[256,8,128]{2,1,0:T(8,128)}), f32[256,8,128]{2,1,0:T(8,128)S(1)}, u32[]{:S(2)}, u32[]{:S(2)}) %all-to-all-start) | async-done | bytes 1048608 | tf_op jit(solution)/shard_map/all_to_all | solution.py:173
  53.9 2.6 %mid.1 = f32[256,8,128]{2,1,0:T(8,128)S(1)} custom-call(f32[256,8,128]{2,1,0:T(8,128)S(1)} %all-to-all-done.x_ref, bf16[4,256,256]{2,1,0:T(8,128)(2,1)S(1)} %get-tuple-element.9.w_high, bf16[4,256,256]{2,1,0:T(8,128)(2,1)S(1)} %get-tuple-element.10.w_low, bf16[256,128]{1,0:T(8,128)(2,1)S(1)} %get-tuple-element.11.m_high, ...), custom_call_target="tpu_custom_call" | custom-call | tf_op jit(solution)/shard_map/mid/pallas_call | solution.py:174
  56.6 37.4 %all_to_all.10 = f32[256,8,128]{2,1,0:T(8,128)S(1)} all-to-all(f32[256,8,128]{2,1,0:T(8,128)S(1)} %mid.1), channel_id=1, replica_groups=mesh['grp'=16,'ing'=16] {'grp','ing'}, dimensions={0} | all-to-all | bytes 2097152 | tf_op jit(solution)/shard_map/all_to_all | solution.py:182
  94.0 1.3 %post.1 = f32[2048,128]{1,0:T(8,128)} custom-call(f32[8,16,2,8,128]{4,3,2,1,0:T(8,128)S(1)} %bitcast.8), custom_call_target="tpu_custom_call" | custom-call | tf_op jit(solution)/shard_map/post/pallas_call | solution.py:183
  (2 shorter events, 0.0 us)
Async XLA Ops:
  0.8 0.7 copy-start.3
  0.8 0.7 copy-start.4
  1.4 1.2 %copy-start = (f32[2,1,1,131072]{3,2,1,0:T(1,128)S(1)}, f32[2,1,1,131072]{3,2,1,0:T(1,128)}, u32[]{:S(2)}) copy-start(f32[2,1,1,131072]{3,2,1,0:T(1,128)} %param.7) | copy-start | bytes 3145732
  2.7 0.8 copy-start.1
  7.4 15.7 %copy-start.5 = (f32[4,2,4,4]{3,2,1,0:T(4,128)S(1)}, f32[4,2,4,4]{3,2,1,0:T(4,128)}, u32[]{:S(2)}) copy-start(f32[4,2,4,4]{3,2,1,0:T(4,128)} %param.12) | copy-start | bytes 1540
  7.4 46.5 %all-to-all-start = ((f32[256,8,128]{2,1,0:T(8,128)}), f32[256,8,128]{2,1,0:T(8,128)S(1)}, u32[]{:S(2)}, u32[]{:S(2)}) async-start(f32[256,8,128]{2,1,0:T(8,128)} %bitcast.1), calls=%async_computation | async-start | bytes 2097152 | tf_op jit(solution)/shard_map/all_to_all | solution.py:173
  23.3 0.8 copy-start.2

commit v2 on v1

v2 whole, which is shorter than its diff:
```python
import jax
import jax.numpy as jnp
from jax import lax
from jax.experimental import pallas as pl
from jax.experimental.pallas import tpu as pltpu
from jax.sharding import PartitionSpec as P

F32 = jnp.float32
BF16 = jnp.bfloat16


def split(value):
    high = value.astype(BF16)
    return high, (value - high.astype(F32)).astype(BF16)


def dot(left, right, dims=((1,), (0,))):
    return lax.dot_general(left, right, (dims, ((), ())), preferred_element_type=F32)


def dot3(left, right, dims=((1,), (0,))):
    (left_high, left_low), (right_high, right_low) = left, right
    return (
        dot(left_high, right_high, dims)
        + dot(left_low, right_high, dims)
        + dot(left_high, right_low, dims)
    )


def prep_kernel(angle_ref, qubit_ref, twist_ref, pair_ref, inner_ref, w_high, w_low, m_high, m_low, turn_ref):
    row = lax.broadcasted_iota(jnp.int32, (256, 8), 0)
    col = lax.broadcasted_iota(jnp.int32, (256, 8), 1)
    r_full = lax.broadcasted_iota(jnp.int32, (256, 256), 0)
    c_full = lax.broadcasted_iota(jnp.int32, (256, 256), 1)
    differ = jnp.bitwise_xor(r_full, c_full)
    for level in range(4):
        key = ((row >> 6) & 1) * 4 + (row >> 7) * 2 + ((row >> level) & 1)
        pick = (key == col).astype(F32).astype(BF16)
        keep = jnp.bitwise_and(differ, 63 - (1 << level)) == 0
        for part, out in zip(split(pair_ref[level]), (w_high, w_low)):
            half = dot(pick, part).astype(BF16)
            out[level] = jnp.where(keep, dot(half, pick, ((1,), (1,))), 0.0).astype(BF16)
    row = lax.broadcasted_iota(jnp.int32, (128, 32), 0)
    col = lax.broadcasted_iota(jnp.int32, (128, 32), 1)
    pick = ((row >> 2) == col).astype(F32).astype(BF16)
    keep = jnp.bitwise_and(differ[:128, :128], 3) == 0
    for c in range(2):
        for part, out in zip(split(inner_ref[c]), (m_high, m_low)):
            half = dot(pick, part).astype(BF16)
            out[c * 128 : c * 128 + 128] = jnp.where(keep, dot(half, pick, ((1,), (1,))), 0.0).astype(BF16)
    base = (lax.axis_index("grp") & 1) * 64 + lax.axis_index("ing") * 4
    sub = lax.broadcasted_iota(jnp.int32, (8, 128), 0)
    lane = lax.broadcasted_iota(jnp.int32, (8, 128), 1)
    position = ((lane & 7) << 7) + (sub & 3) + base
    phases = jnp.zeros((8, 128), F32)
    for qubit in range(10):
        phases = phases + angle_ref[qubit] * (1 - 2 * ((position >> qubit) & 1)).astype(F32)
    for entry in range(16):
        first_bit = lax.shift_right_logical(position, jnp.full((8, 128), qubit_ref[0, entry], jnp.int32))
        second_bit = lax.shift_right_logical(position, jnp.full((8, 128), qubit_ref[1, entry], jnp.int32))
        odd = jnp.bitwise_and(jnp.bitwise_xor(first_bit, second_bit), 1)
        phases = phases + twist_ref[entry] * (1 - 2 * odd).astype(F32)
    turn_ref[0] = jnp.cos(phases)
    turn_ref[1] = jnp.sin(phases)


def pre_kernel(x_hbm, gate_hbm, z_ref, x_ref, gate_ref, y_ref, in_sems):
    fetch_gates = pltpu.make_async_copy(gate_hbm, gate_ref, in_sems.at[4])
    fetch_gates.start()
    x_view = x_ref.reshape(64, 32, 128)
    fetches = [
        pltpu.make_async_copy(x_hbm.at[:, pl.ds(8 * j, 8), :], x_view.at[:, pl.ds(8 * j, 8), :], in_sems.at[j])
        for j in range(4)
    ]
    for fetch in fetches:
        fetch.start()
    fetch_gates.wait()
    real, imag = gate_ref[0, 0], gate_ref[0, 1]
    first = split(jnp.concatenate([jnp.concatenate([real, -imag], 1), jnp.concatenate([imag, real], 1)], 0))
    real, imag = gate_ref[1, 0], gate_ref[1, 1]
    zero = jnp.zeros_like(real)
    rows = [
        [real, zero, -imag, zero],
        [zero, real, zero, -imag],
        [imag, zero, real, zero],
        [zero, imag, zero, real],
    ]
    second = split(jnp.concatenate([jnp.concatenate(r, 1) for r in rows], 0).T)
    for j in range(4):
        fetches[j].wait()
        columns = [x_ref[pl.ds(8 * j + b, 64, stride=32), :] for b in range(8)]
        result = dot3(first, split(jnp.concatenate(columns, 1)))
        for b in range(8):
            at = (8 * j + b) * 64
            y_ref[at : at + 64] = result[:, b * 128 : b * 128 + 128]
    sub = lax.broadcasted_iota(jnp.int32, (16, 8, 128), 1)
    for ah in range(8):
        halves = []
        for top in range(2):
            a = (top * 8 + ah) * 2
            x = jnp.concatenate([y_ref[pl.ds(c * 32 + a + q, 32, stride=64), :] for c in range(2) for q in range(2)], 0)
            halves.append(dot3(split(x.T), second).reshape(16, 8, 128))
        z0, z1 = halves
        z_ref[ah, :, 0] = jnp.where(sub < 4, z0, pltpu.roll(z1, 4, 1))
        z_ref[ah, :, 1] = jnp.where(sub < 4, pltpu.roll(z0, 4, 1), z1)


def mid_kernel(x_ref, w_high, w_low, m_high, m_low, turn_ref, out_ref):
    inner = (m_high[...], m_low[...])
    lane = lax.broadcasted_iota(jnp.int32, (128, 128), 1)
    cosine, sine = turn_ref[0], turn_ref[1]
    parts = []
    for g in range(16):
        u = dot3(inner, split(x_ref[g * 16 : g * 16 + 16].reshape(128, 128)))
        real, imag = u[:128].reshape(16, 8, 128), u[128:].reshape(16, 8, 128)
        kept = cosine * real - sine * imag
        turned = pltpu.roll((cosine * imag + sine * real).reshape(128, 128), 64, 1)
        parts.append(kept.reshape(128, 128) + jnp.where(lane < 64, -turned, turned))
    for level in range(4):
        weight = (w_high[level], w_low[level])
        new = [None] * 16
        for g in range(16):
            if g >> level & 1:
                continue
            h = g | 1 << level
            y = dot3(split(jnp.concatenate([parts[g], parts[h]], 1)), weight)
            new[g], new[h] = y[:, :128], y[:, 128:]
        parts = new
    for g in range(16):
        out_ref[g * 16 : g * 16 + 16] = parts[g].reshape(16, 8, 128)


def post_kernel(x_ref, out_hbm, z_ref, sems):
    sub = lax.broadcasted_iota(jnp.int32, (16, 8, 128), 1)
    sends = []
    for ah in range(8):
        even, odd = x_ref[ah, :, 0], x_ref[ah, :, 1]
        z0 = jnp.where(sub < 4, even, pltpu.roll(odd, 4, 1)).reshape(128, 128)
        z1 = jnp.where(sub < 4, pltpu.roll(even, 4, 1), odd).reshape(128, 128)
        for top, z in enumerate((z0, z1)):
            a = top * 8 + ah
            turned = z.T
            for c in range(2):
                at = c * 1024 + a * 64
                z_ref[at : at + 64] = turned[c * 64 : c * 64 + 64]
                send = pltpu.make_async_copy(
                    z_ref.at[pl.ds(at, 64)], out_hbm.at[pl.ds(at, 64)], sems.at[c * 16 + a]
                )
                send.start()
                sends.append(send)
    for send in sends:
        send.wait()


SMEM = pl.BlockSpec(memory_space=pltpu.SMEM)
VMEM = pl.BlockSpec(memory_space=pltpu.VMEM)
HBM = pl.BlockSpec(memory_space=pltpu.HBM)
PARAMS = pltpu.CompilerParams(vmem_limit_bytes=48 << 20)


def on_device(state_vector, local_gates, local_angles, pair_qubits, pair_angles, group_gates, inner_gate):
    turned = group_gates.transpose(0, 1, 3, 2)
    real, imag = turned[:, 0], turned[:, 1]
    pairs = jnp.concatenate([jnp.concatenate([real, imag], 2), jnp.concatenate([-imag, real], 2)], 1)
    weights = pl.pallas_call(
        prep_kernel,
        out_shape=(
            jax.ShapeDtypeStruct((4, 256, 256), BF16),
            jax.ShapeDtypeStruct((4, 256, 256), BF16),
            jax.ShapeDtypeStruct((256, 128), BF16),
            jax.ShapeDtypeStruct((256, 128), BF16),
            jax.ShapeDtypeStruct((2, 8, 128), F32),
        ),
        in_specs=[SMEM, SMEM, SMEM, VMEM, VMEM],
        out_specs=(VMEM,) * 5,
        compiler_params=PARAMS,
        name="prep",
    )(local_angles, pair_qubits.T, pair_angles, pairs, inner_gate)
    sent = pl.pallas_call(
        pre_kernel,
        out_shape=pltpu.VMEM((8, 16, 2, 8, 128), F32),
        in_specs=[HBM, HBM],
        out_specs=VMEM,
        scratch_shapes=[
            pltpu.VMEM((2048, 128), F32),
            pltpu.VMEM((2, 2, 32, 32), F32),
            pltpu.VMEM((2048, 128), F32),
            pltpu.SemaphoreType.DMA((5,)),
        ],
        compiler_params=PARAMS,
        name="pre",
    )(
        pltpu.with_memory_space_constraint(state_vector.reshape(64, 32, 128), pltpu.HBM),
        pltpu.with_memory_space_constraint(local_gates, pltpu.HBM),
    )
    held = lax.all_to_all(sent.reshape(256, 8, 128), ("grp", "ing"), 0, 0, tiled=True)
    done = pl.pallas_call(
        mid_kernel,
        out_shape=jax.ShapeDtypeStruct((256, 8, 128), F32),
        in_specs=[VMEM] * 6,
        out_specs=VMEM,
        compiler_params=PARAMS,
        name="mid",
    )(held, *weights)
    back = lax.all_to_all(done, ("grp", "ing"), 0, 0, tiled=True)
    out = pl.pallas_call(
        post_kernel,
        out_shape=jax.ShapeDtypeStruct((2048, 128), F32),
        in_specs=[VMEM],
        out_specs=HBM,
        scratch_shapes=[pltpu.VMEM((2048, 128), F32), pltpu.SemaphoreType.DMA((32,))],
        compiler_params=PARAMS,
        name="post",
    )(back.reshape(8, 16, 2, 8, 128))
    return out.reshape(state_vector.shape)


def solution(mesh):
    return jax.shard_map(
        on_device,
        mesh=mesh,
        in_specs=(P(None, "grp", "ing", None), P(), P(), P(), P(), P(), P()),
        out_specs=P(None, "grp", "ing", None),
        check_vma=False,
    )
```

time: 95.6 us -> 92.6 us (0.969)
  local copies, waits for them, and re-layouts: 4.39 us -> 0.92 us
  Pallas kernels: 9.2 us -> 10.3 us
    unnamed x13 -> x10, local copies, waits for them, and re-layouts: 4.16 us -> 0.69 us
  transfers between devices with their start and end apart: 1 -> 1, of which waited for: 1 -> 1; matrix products, arithmetic and copies ran while one was open for 0% -> 0% of each run, Pallas kernels for 1% -> 2%
where the time goes in v2:
time: 92.6 us; the launch traced here: 92.3 us
  blocking collectives  37.4 us (40%)
  waiting for transfers between devices  27.9 us (30%)
  starting transfers between devices  15.7 us (17%)
  Pallas kernels  10.3 us (11%)
    all_to_all x1, blocking collectives, on_device(): back = lax.all_to_all(done, ('grp', 'ing'), 0, 0, tiled=True)  37.4 us
    all_to_all x1, waiting for transfers between devices, on_device(): lax.all_to_all(sent.reshape(256, 8, 128), ('grp', 'ing'), 0, 0, tiled=True)  27.9 us
    all_to_all x1, starting transfers between devices, on_device(): lax.all_to_all(sent.reshape(256, 8, 128), ('grp', 'ing'), 0, 0, tiled=True)  15.7 us
    pallas_call x1, Pallas kernels, on_device(): pl.pallas_call(pre_kernel, out_shape=pltpu.VMEM((8, 16, 2, 8, 128), F32),...  4.43 us
    pallas_call x1, Pallas kernels, on_device(): pl.pallas_call(mid_kernel, out_shape=jax.ShapeDtypeStruct((256, 8, 128),...  2.68 us
    pallas_call x1, Pallas kernels, on_device(): pl.pallas_call(prep_kernel, out_shape=(jax.ShapeDtypeStruct((4, 256, 256)...  1.88 us
  transfers between devices with their start and end apart: 1, of which 1 were waited for; matrix products, arithmetic and copies ran while one was open for 0% of the time, Pallas kernels for 2%

profile of v2, /device:TPU:1, one launch (start us, length us, event | category | flops | bytes accessed | tf_op | source)
XLA Modules:
  0.0 92.3 jit_solution(10156511779870964323)
XLA Ops:
  0.0 4.4 %pre.1 = f32[8,16,2,8,128]{4,3,2,1,0:T(8,128)} custom-call(f32[64,32,128]{2,1,0:T(8,128)} %bitcast.11, f32[2,2,32,32]{3,2,1,0:T(8,128)} %gate_hbm.1), custom_call_target="tpu_custom_call" | custom-call | tf_op jit(solution)/shard_map/pre/pallas_call | solution.py:179
  4.4 0.0 copy-start.4
  4.5 15.7 %all-to-all-start = ((f32[256,8,128]{2,1,0:T(8,128)}), f32[256,8,128]{2,1,0:T(8,128)S(1)}, u32[]{:S(2)}, u32[]{:S(2)}) async-start(f32[256,8,128]{2,1,0:T(8,128)} %bitcast.1), calls=%async_computation | async-start | bytes 2097152 | tf_op jit(solution)/shard_map/all_to_all | solution.py:196
  20.1 0.0 copy-done.4
  20.1 0.1 copy.9
  20.2 0.1 copy.8
  20.4 0.0 copy-start
  20.4 0.0 copy-start.3
  20.4 0.1 maximum_maximum_fusion.pair_ref
  20.5 0.0 copy-start.1
  20.5 0.0 copy-start.2
  20.5 0.7 copy-done
  21.1 0.0 copy-done.3
  21.1 0.0 copy-done.1
  21.1 0.0 copy-done.2
  21.1 1.9 %prep.1 = (bf16[4,256,256]{2,1,0:T(8,128)(2,1)S(1)}, bf16[4,256,256]{2,1,0:T(8,128)(2,1)S(1)}, bf16[256,128]{1,0:T(8,128)(2,1)S(1)}, bf16[256,128]{1,0:T(8,128)(2,1)S(1)}, f32[2,8,128]{2,1,0:T(8,128)S(1)}) custom-call(f32[10]{0:T(128)S(1)} %copy-done.2, s32[2,16]{1,0:T(2,128)S(1)} %bitcast.10, f32[16]{0:T(128)S(1)} %copy-done.3, ...), custom_call_target="tpu_custom_call" | custom-call | tf_op jit(solution)/shard_map/prep/pallas_call | solution.py:165
  23.0 27.9 %all-to-all-done.x_ref = f32[256,8,128]{2,1,0:T(8,128)S(1)} async-done(((f32[256,8,128]{2,1,0:T(8,128)}), f32[256,8,128]{2,1,0:T(8,128)S(1)}, u32[]{:S(2)}, u32[]{:S(2)}) %all-to-all-start) | async-done | bytes 1048608 | tf_op jit(solution)/shard_map/all_to_all | solution.py:196
  50.9 2.7 %mid.1 = f32[256,8,128]{2,1,0:T(8,128)S(1)} custom-call(f32[256,8,128]{2,1,0:T(8,128)S(1)} %all-to-all-done.x_ref, bf16[4,256,256]{2,1,0:T(8,128)(2,1)S(1)} %get-tuple-element.10.w_high, bf16[4,256,256]{2,1,0:T(8,128)(2,1)S(1)} %get-tuple-element.11.w_low, bf16[256,128]{1,0:T(8,128)(2,1)S(1)} %get-tuple-element.12.m_high, ...), custom_call_target="tpu_custom_call" | custom-call | tf_op jit(solution)/shard_map/mid/pallas_call | solution.py:197
  53.6 37.4 %all_to_all.10 = f32[256,8,128]{2,1,0:T(8,128)S(1)} all-to-all(f32[256,8,128]{2,1,0:T(8,128)S(1)} %mid.1), channel_id=1, replica_groups=mesh['grp'=16,'ing'=16] {'grp','ing'}, dimensions={0} | all-to-all | bytes 2097152 | tf_op jit(solution)/shard_map/all_to_all | solution.py:205
  91.0 1.3 %post.1 = f32[2048,128]{1,0:T(8,128)} custom-call(f32[8,16,2,8,128]{4,3,2,1,0:T(8,128)S(1)} %bitcast.9), custom_call_target="tpu_custom_call" | custom-call | tf_op jit(solution)/shard_map/post/pallas_call | solution.py:206
  (2 shorter events, 0.0 us)
Async XLA Ops:
  4.4 15.7 %copy-start.4 = (f32[4,2,4,4]{3,2,1,0:T(4,128)S(1)}, f32[4,2,4,4]{3,2,1,0:T(4,128)}, u32[]{:S(2)}) copy-start(f32[4,2,4,4]{3,2,1,0:T(4,128)} %param.12) | copy-start | bytes 1540
  4.5 46.5 %all-to-all-start = ((f32[256,8,128]{2,1,0:T(8,128)}), f32[256,8,128]{2,1,0:T(8,128)S(1)}, u32[]{:S(2)}, u32[]{:S(2)}) async-start(f32[256,8,128]{2,1,0:T(8,128)} %bitcast.1), calls=%async_computation | async-start | bytes 2097152 | tf_op jit(solution)/shard_map/all_to_all | solution.py:196
  20.4 0.8 copy-start
  20.4 0.8 copy-start.3
  20.5 0.7 copy-start.1
  20.5 0.7 copy-start.2

commit v3 on v2

--- a/solution.py
+++ b/solution.py
@@ -33,13 +33,21 @@
     r_full = lax.broadcasted_iota(jnp.int32, (256, 256), 0)
     c_full = lax.broadcasted_iota(jnp.int32, (256, 256), 1)
     differ = jnp.bitwise_xor(r_full, c_full)
-    for level in range(4):
-        key = ((row >> 6) & 1) * 4 + (row >> 7) * 2 + ((row >> level) & 1)
-        pick = (key == col).astype(F32).astype(BF16)
-        keep = jnp.bitwise_and(differ, 63 - (1 << level)) == 0
-        for part, out in zip(split(pair_ref[level]), (w_high, w_low)):
-            half = dot(pick, part).astype(BF16)
-            out[level] = jnp.where(keep, dot(half, pick, ((1,), (1,))), 0.0).astype(BF16)
+    for high in range(2):
+        halves = []
+        for n in range(2):
+            level = 2 * high + n
+            group = (row >> 7) if n else (row >> 5) & 1
+            key = ((row >> 6) & 1) * 4 + group * 2 + ((row >> level) & 1)
+            pick = (key == col).astype(F32).astype(BF16)
+            others = 255 - (64 + (128 if n else 32) + (1 << level))
+            keep = jnp.bitwise_and(differ, others) == 0
+            spread = []
+            for part in split(pair_ref[level]):
+                half = dot(pick, part).astype(BF16)
+                spread.append(jnp.where(keep, dot(half, pick, ((1,), (1,))), 0.0).astype(BF16))
+            halves.append(spread)
+        w_high[high], w_low[high] = split(dot3(*halves))
     row = lax.broadcasted_iota(jnp.int32, (128, 32), 0)
     col = lax.broadcasted_iota(jnp.int32, (128, 32), 1)
     pick = ((row >> 2) == col).astype(F32).astype(BF16)
@@ -64,16 +72,11 @@
     turn_ref[1] = jnp.sin(phases)
 
 
-def pre_kernel(x_hbm, gate_hbm, z_ref, x_ref, gate_ref, y_ref, in_sems):
-    fetch_gates = pltpu.make_async_copy(gate_hbm, gate_ref, in_sems.at[4])
+def pre_kernel(x_hbm, gate_hbm, out_hbm, x_ref, gate_ref, y_ref, z_ref, in_sems, out_sems):
+    fetch_gates = pltpu.make_async_copy(gate_hbm, gate_ref, in_sems.at[0])
     fetch_gates.start()
-    x_view = x_ref.reshape(64, 32, 128)
-    fetches = [
-        pltpu.make_async_copy(x_hbm.at[:, pl.ds(8 * j, 8), :], x_view.at[:, pl.ds(8 * j, 8), :], in_sems.at[j])
-        for j in range(4)
-    ]
-    for fetch in fetches:
-        fetch.start()
+    fetch = pltpu.make_async_copy(x_hbm, x_ref, in_sems.at[1])
+    fetch.start()
     fetch_gates.wait()
     real, imag = gate_ref[0, 0], gate_ref[0, 1]
     first = split(jnp.concatenate([jnp.concatenate([real, -imag], 1), jnp.concatenate([imag, real], 1)], 0))
@@ -86,14 +89,15 @@
         [zero, imag, zero, real],
     ]
     second = split(jnp.concatenate([jnp.concatenate(r, 1) for r in rows], 0).T)
+    fetch.wait()
     for j in range(4):
-        fetches[j].wait()
         columns = [x_ref[pl.ds(8 * j + b, 64, stride=32), :] for b in range(8)]
         result = dot3(first, split(jnp.concatenate(columns, 1)))
         for b in range(8):
             at = (8 * j + b) * 64
             y_ref[at : at + 64] = result[:, b * 128 : b * 128 + 128]
     sub = lax.broadcasted_iota(jnp.int32, (16, 8, 128), 1)
+    sends = []
     for ah in range(8):
         halves = []
         for top in range(2):
@@ -103,6 +107,10 @@
         z0, z1 = halves
         z_ref[ah, :, 0] = jnp.where(sub < 4, z0, pltpu.roll(z1, 4, 1))
         z_ref[ah, :, 1] = jnp.where(sub < 4, pltpu.roll(z0, 4, 1), z1)
+        sends.append(pltpu.make_async_copy(z_ref.at[ah], out_hbm.at[ah], out_sems.at[ah]))
+        sends[-1].start()
+    for send in sends:
+        send.wait()
 
 
 def mid_kernel(x_ref, w_high, w_low, m_high, m_low, turn_ref, out_ref):
@@ -116,18 +124,31 @@
         kept = cosine * real - sine * imag
         turned = pltpu.roll((cosine * imag + sine * real).reshape(128, 128), 64, 1)
         parts.append(kept.reshape(128, 128) + jnp.where(lane < 64, -turned, turned))
-    for level in range(4):
-        weight = (w_high[level], w_low[level])
-        new = [None] * 16
-        for g in range(16):
-            if g >> level & 1:
-                continue
-            h = g | 1 << level
-            y = dot3(split(jnp.concatenate([parts[g], parts[h]], 1)), weight)
-            new[g], new[h] = y[:, :128], y[:, 128:]
-        parts = new
-    for g in range(16):
-        out_ref[g * 16 : g * 16 + 16] = parts[g].reshape(16, 8, 128)
+    low = (lane & 32) == 0
+
+    def trade(first, second):
+        return (
+            jnp.where(low, first, pltpu.roll(second, 32, 1)),
+            jnp.where(low, pltpu.roll(first, 96, 1), second),
+        )
+
+    def joined(first, second, level):
+        y = dot3(split(jnp.concatenate([first, second], 1)), (w_high[level], w_low[level]))
+        return y[:, :128], y[:, 128:]
+
+    for g in range(0, 16, 2):
+        parts[g], parts[g + 1] = trade(parts[g], parts[g + 1])
+    for g in (0, 1, 4, 5, 8, 9, 12, 13):
+        parts[g], parts[g + 2] = joined(parts[g], parts[g + 2], 0)
+    for g in (0, 1, 2, 3, 8, 9, 10, 11):
+        parts[g], parts[g + 4] = trade(parts[g], parts[g + 4])
+    for g in range(8):
+        parts[g], parts[g + 8] = joined(parts[g], parts[g + 8], 1)
+    for g in range(0, 16, 2):
+        parts[g], parts[g + 1] = trade(parts[g], parts[g + 1])
+    for slot in range(16):
+        g = (slot & 8) | (slot & 2) | ((slot & 1) << 2) | ((slot >> 2) & 1)
+        out_ref[g * 16 : g * 16 + 16] = parts[slot].reshape(16, 8, 128)
 
 
 def post_kernel(x_ref, out_hbm, z_ref, sems):
@@ -138,16 +159,12 @@
         z0 = jnp.where(sub < 4, even, pltpu.roll(odd, 4, 1)).reshape(128, 128)
         z1 = jnp.where(sub < 4, pltpu.roll(even, 4, 1), odd).reshape(128, 128)
         for top, z in enumerate((z0, z1)):
-            a = top * 8 + ah
             turned = z.T
             for c in range(2):
-                at = c * 1024 + a * 64
-                z_ref[at : at + 64] = turned[c * 64 : c * 64 + 64]
-                send = pltpu.make_async_copy(
-                    z_ref.at[pl.ds(at, 64)], out_hbm.at[pl.ds(at, 64)], sems.at[c * 16 + a]
-                )
-                send.start()
-                sends.append(send)
+                z_ref[c, top, ah] = turned[c * 64 : c * 64 + 64]
+        send = pltpu.make_async_copy(z_ref.at[:, :, ah], out_hbm.at[:, :, ah], sems.at[ah])
+        send.start()
+        sends.append(send)
     for send in sends:
         send.wait()
 
@@ -165,8 +182,8 @@
     weights = pl.pallas_call(
         prep_kernel,
         out_shape=(
-            jax.ShapeDtypeStruct((4, 256, 256), BF16),
-            jax.ShapeDtypeStruct((4, 256, 256), BF16),
+            jax.ShapeDtypeStruct((2, 256, 256), BF16),
+            jax.ShapeDtypeStruct((2, 256, 256), BF16),
             jax.ShapeDtypeStruct((256, 128), BF16),
             jax.ShapeDtypeStruct((256, 128), BF16),
             jax.ShapeDtypeStruct((2, 8, 128), F32),
@@ -178,19 +195,21 @@
     )(local_angles, pair_qubits.T, pair_angles, pairs, inner_gate)
     sent = pl.pallas_call(
         pre_kernel,
-        out_shape=pltpu.VMEM((8, 16, 2, 8, 128), F32),
+        out_shape=pltpu.HBM((8, 16, 2, 8, 128), F32),
         in_specs=[HBM, HBM],
-        out_specs=VMEM,
+        out_specs=HBM,
         scratch_shapes=[
             pltpu.VMEM((2048, 128), F32),
             pltpu.VMEM((2, 2, 32, 32), F32),
             pltpu.VMEM((2048, 128), F32),
-            pltpu.SemaphoreType.DMA((5,)),
+            pltpu.VMEM((8, 16, 2, 8, 128), F32),
+            pltpu.SemaphoreType.DMA((2,)),
+            pltpu.SemaphoreType.DMA((8,)),
         ],
         compiler_params=PARAMS,
         name="pre",
     )(
-        pltpu.with_memory_space_constraint(state_vector.reshape(64, 32, 128), pltpu.HBM),
+        pltpu.with_memory_space_constraint(state_vector.reshape(2048, 128), pltpu.HBM),
         pltpu.with_memory_space_constraint(local_gates, pltpu.HBM),
     )
     held = lax.all_to_all(sent.reshape(256, 8, 128), ("grp", "ing"), 0, 0, tiled=True)
@@ -205,10 +224,10 @@
     back = lax.all_to_all(done, ("grp", "ing"), 0, 0, tiled=True)
     out = pl.pallas_call(
         post_kernel,
-        out_shape=jax.ShapeDtypeStruct((2048, 128), F32),
+        out_shape=pltpu.HBM((2, 2, 8, 64, 128), F32),
         in_specs=[VMEM],
         out_specs=HBM,
-        scratch_shapes=[pltpu.VMEM((2048, 128), F32), pltpu.SemaphoreType.DMA((32,))],
+        scratch_shapes=[pltpu.VMEM((2, 2, 8, 64, 128), F32), pltpu.SemaphoreType.DMA((8,))],
         compiler_params=PARAMS,
         name="post",
     )(back.reshape(8, 16, 2, 8, 128))

time: 92.6 us -> 91.4 us (0.987)
  transfers between devices with their start and end apart: 1 -> 1, of which waited for: 1 -> 1; matrix products, arithmetic and copies ran while one was open for 0% -> 0% of each run, Pallas kernels for 2% -> 3%
where the time goes in v3:
time: 91.4 us; the launch traced here: 91.1 us
  blocking collectives  37.4 us (41%)
  waiting for transfers between devices  27.4 us (30%)
  starting transfers between devices  15.7 us (17%)
  Pallas kernels  9.55 us (10%)
  local copies, waits for them, and re-layouts  0.92 us (1%)
    all_to_all x1, blocking collectives, on_device(): back = lax.all_to_all(done, ('grp', 'ing'), 0, 0, tiled=True)  37.4 us
    all_to_all x1, waiting for transfers between devices, on_device(): lax.all_to_all(sent.reshape(256, 8, 128), ('grp', 'ing'), 0, 0, tiled=True)  27.4 us
    all_to_all x1, starting transfers between devices, on_device(): lax.all_to_all(sent.reshape(256, 8, 128), ('grp', 'ing'), 0, 0, tiled=True)  15.7 us
    pallas_call x1, Pallas kernels, on_device(): pl.pallas_call(pre_kernel, out_shape=pltpu.HBM((8, 16, 2, 8, 128), F32),...  3.89 us
    pallas_call x1, Pallas kernels, on_device(): pl.pallas_call(prep_kernel, out_shape=(jax.ShapeDtypeStruct((2, 256, 256)...  2.32 us
    pallas_call x1, Pallas kernels, on_device(): pl.pallas_call(mid_kernel, out_shape=jax.ShapeDtypeStruct((256, 8, 128),...  2.21 us
  transfers between devices with their start and end apart: 1, of which 1 were waited for; matrix products, arithmetic and copies ran while one was open for 0% of the time, Pallas kernels for 3%

profile of v3, /device:TPU:1, one launch (start us, length us, event | category | flops | bytes accessed | tf_op | source)
XLA Modules:
  0.0 91.1 jit_solution(6775249480423343335)
XLA Ops:
  0.0 3.9 %pre.1 = f32[8,16,2,8,128]{4,3,2,1,0:T(8,128)} custom-call(f32[2048,128]{1,0:T(8,128)} %bitcast.12, f32[2,2,32,32]{3,2,1,0:T(8,128)} %gate_hbm.1), custom_call_target="tpu_custom_call" | custom-call | tf_op jit(solution)/shard_map/pre/pallas_call | solution.py:196
  3.9 0.0 copy-start.4
  3.9 15.7 %all-to-all-start = ((f32[256,8,128]{2,1,0:T(8,128)}), f32[256,8,128]{2,1,0:T(8,128)S(1)}, u32[]{:S(2)}, u32[]{:S(2)}) async-start(f32[256,8,128]{2,1,0:T(8,128)} %bitcast.11), calls=%async_computation | async-start | bytes 2097152 | tf_op jit(solution)/shard_map/all_to_all | solution.py:215
  19.6 0.0 copy-done.4
  19.6 0.1 copy.8
  19.7 0.1 copy.9
  19.8 0.0 copy-start
  19.8 0.0 copy-start.3
  19.8 0.1 maximum_maximum_fusion.pair_ref
  19.9 0.0 copy-start.1
  19.9 0.0 copy-start.2
  19.9 0.7 copy-done
  20.6 0.0 copy-done.3
  20.6 0.0 copy-done.1
  20.6 0.0 copy-done.2
  20.6 2.3 %prep.1 = (bf16[2,256,256]{2,1,0:T(8,128)(2,1)S(1)}, bf16[2,256,256]{2,1,0:T(8,128)(2,1)S(1)}, bf16[256,128]{1,0:T(8,128)(2,1)S(1)}, bf16[256,128]{1,0:T(8,128)(2,1)S(1)}, f32[2,8,128]{2,1,0:T(8,128)S(1)}) custom-call(f32[10]{0:T(128)S(1)} %copy-done.2, s32[2,16]{1,0:T(2,128)S(1)} %bitcast.10, f32[16]{0:T(128)S(1)} %copy-done.3, ...), custom_call_target="tpu_custom_call" | custom-call | tf_op jit(solution)/shard_map/prep/pallas_call | solution.py:182
  22.9 27.4 %all-to-all-done.x_ref = f32[256,8,128]{2,1,0:T(8,128)S(1)} async-done(((f32[256,8,128]{2,1,0:T(8,128)}), f32[256,8,128]{2,1,0:T(8,128)S(1)}, u32[]{:S(2)}, u32[]{:S(2)}) %all-to-all-start) | async-done | bytes 1048608 | tf_op jit(solution)/shard_map/all_to_all | solution.py:215
  50.4 2.2 %mid.1 = f32[256,8,128]{2,1,0:T(8,128)S(1)} custom-call(f32[256,8,128]{2,1,0:T(8,128)S(1)} %all-to-all-done.x_ref, bf16[2,256,256]{2,1,0:T(8,128)(2,1)S(1)} %get-tuple-element.10.w_high, bf16[2,256,256]{2,1,0:T(8,128)(2,1)S(1)} %get-tuple-element.11.w_low, bf16[256,128]{1,0:T(8,128)(2,1)S(1)} %get-tuple-element.12.m_high, ...), custom_call_target="tpu_custom_call" | custom-call | tf_op jit(solution)/shard_map/mid/pallas_call | solution.py:216
  52.6 37.4 %all_to_all.10 = f32[256,8,128]{2,1,0:T(8,128)S(1)} all-to-all(f32[256,8,128]{2,1,0:T(8,128)S(1)} %mid.1), channel_id=1, replica_groups=mesh['grp'=16,'ing'=16] {'grp','ing'}, dimensions={0} | all-to-all | bytes 2097152 | tf_op jit(solution)/shard_map/all_to_all | solution.py:224
  90.0 1.1 %post.1 = f32[2,2,8,64,128]{4,3,2,1,0:T(8,128)} custom-call(f32[8,16,2,8,128]{4,3,2,1,0:T(8,128)S(1)} %bitcast.9), custom_call_target="tpu_custom_call" | custom-call | tf_op jit(solution)/shard_map/post/pallas_call | solution.py:225
  (2 shorter events, 0.0 us)
Async XLA Ops:
  3.9 15.7 %copy-start.4 = (f32[4,2,4,4]{3,2,1,0:T(4,128)S(1)}, f32[4,2,4,4]{3,2,1,0:T(4,128)}, u32[]{:S(2)}) copy-start(f32[4,2,4,4]{3,2,1,0:T(4,128)} %param.12) | copy-start | bytes 1540
  3.9 46.5 %all-to-all-start = ((f32[256,8,128]{2,1,0:T(8,128)}), f32[256,8,128]{2,1,0:T(8,128)S(1)}, u32[]{:S(2)}, u32[]{:S(2)}) async-start(f32[256,8,128]{2,1,0:T(8,128)} %bitcast.11), calls=%async_computation | async-start | bytes 2097152 | tf_op jit(solution)/shard_map/all_to_all | solution.py:215
  19.8 0.8 copy-start
  19.8 0.8 copy-start.3
  19.9 0.7 copy-start.1
  19.9 0.7 copy-start.2

commit v4 on v3

--- a/solution.py
+++ b/solution.py
@@ -55,7 +55,7 @@
     for c in range(2):
         for part, out in zip(split(inner_ref[c]), (m_high, m_low)):
             half = dot(pick, part).astype(BF16)
-            out[c * 128 : c * 128 + 128] = jnp.where(keep, dot(half, pick, ((1,), (1,))), 0.0).astype(BF16)
+            out[:, c * 128 : c * 128 + 128] = jnp.where(keep, dot(half, pick, ((1,), (1,))), 0.0).astype(BF16)
     base = (lax.axis_index("grp") & 1) * 64 + lax.axis_index("ing") * 4
     sub = lax.broadcasted_iota(jnp.int32, (8, 128), 0)
     lane = lax.broadcasted_iota(jnp.int32, (8, 128), 1)
@@ -89,10 +89,13 @@
         [zero, imag, zero, real],
     ]
     second = split(jnp.concatenate([jnp.concatenate(r, 1) for r in rows], 0).T)
+    first_high, first_low = first
+    stacked = jnp.concatenate([first_high, first_low, first_high], 1)
     fetch.wait()
     for j in range(4):
         columns = [x_ref[pl.ds(8 * j + b, 64, stride=32), :] for b in range(8)]
-        result = dot3(first, split(jnp.concatenate(columns, 1)))
+        high, rest = split(jnp.concatenate(columns, 1))
+        result = dot(stacked, jnp.concatenate([high, high, rest], 0))
         for b in range(8):
             at = (8 * j + b) * 64
             y_ref[at : at + 64] = result[:, b * 128 : b * 128 + 128]
@@ -117,13 +120,19 @@
     inner = (m_high[...], m_low[...])
     lane = lax.broadcasted_iota(jnp.int32, (128, 128), 1)
     cosine, sine = turn_ref[0], turn_ref[1]
+    sign = jnp.where(lane[:8] < 64, -1.0, 1.0)
+    cosine_i, sine_i = cosine * sign, sine * sign
     parts = []
-    for g in range(16):
-        u = dot3(inner, split(x_ref[g * 16 : g * 16 + 16].reshape(128, 128)))
-        real, imag = u[:128].reshape(16, 8, 128), u[128:].reshape(16, 8, 128)
-        kept = cosine * real - sine * imag
-        turned = pltpu.roll((cosine * imag + sine * real).reshape(128, 128), 64, 1)
-        parts.append(kept.reshape(128, 128) + jnp.where(lane < 64, -turned, turned))
+    for start in range(0, 16, 2):
+        columns = []
+        for g in range(start, start + 2):
+            x = x_ref[g * 16 : g * 16 + 16]
+            swapped = pltpu.roll(x.reshape(128, 128), 64, 1).reshape(16, 8, 128)
+            third = cosine * x + sine_i * swapped
+            third_i = cosine_i * swapped - sine * x
+            columns.append(jnp.concatenate([third.reshape(128, 128), third_i.reshape(128, 128)], 0))
+        u = dot3(inner, split(jnp.concatenate(columns, 1)))
+        parts += [u[:, :128], u[:, 128:]]
     low = (lane & 32) == 0
 
     def trade(first, second):
@@ -184,8 +193,8 @@
         out_shape=(
             jax.ShapeDtypeStruct((2, 256, 256), BF16),
             jax.ShapeDtypeStruct((2, 256, 256), BF16),
-            jax.ShapeDtypeStruct((256, 128), BF16),
-            jax.ShapeDtypeStruct((256, 128), BF16),
+            jax.ShapeDtypeStruct((128, 256), BF16),
+            jax.ShapeDtypeStruct((128, 256), BF16),
             jax.ShapeDtypeStruct((2, 8, 128), F32),
         ),
         in_specs=[SMEM, SMEM, SMEM, VMEM, VMEM],

time: 91.4 us -> 91 us (level)
  no operation moved by 1% of the time
where the time goes in v4:
time: 91 us; the launch traced here: 90.7 us
  blocking collectives  37.4 us (41%)
  waiting for transfers between devices  27.5 us (30%)
  starting transfers between devices  15.7 us (17%)
  Pallas kernels  9.1 us (10%)
  local copies, waits for them, and re-layouts  0.92 us (1%)
    all_to_all x1, blocking collectives, on_device(): back = lax.all_to_all(done, ('grp', 'ing'), 0, 0, tiled=True)  37.4 us
    all_to_all x1, waiting for transfers between devices, on_device(): lax.all_to_all(sent.reshape(256, 8, 128), ('grp', 'ing'), 0, 0, tiled=True)  27.5 us
    all_to_all x1, starting transfers between devices, on_device(): lax.all_to_all(sent.reshape(256, 8, 128), ('grp', 'ing'), 0, 0, tiled=True)  15.7 us
    pallas_call x1, Pallas kernels, on_device(): pl.pallas_call(pre_kernel, out_shape=pltpu.HBM((8, 16, 2, 8, 128), F32),...  3.64 us
    pallas_call x1, Pallas kernels, on_device(): pl.pallas_call(prep_kernel, out_shape=(jax.ShapeDtypeStruct((2, 256, 256)...  2.32 us
    pallas_call x1, Pallas kernels, on_device(): pl.pallas_call(mid_kernel, out_shape=jax.ShapeDtypeStruct((256, 8, 128),...  2.01 us
  transfers between devices with their start and end apart: 1, of which 1 were waited for; matrix products, arithmetic and copies ran while one was open for 0% of the time, Pallas kernels for 3%

profile of v4, /device:TPU:1, one launch (start us, length us, event | category | flops | bytes accessed | tf_op | source)
XLA Modules:
  0.0 90.7 jit_solution(12980956962225981811)
XLA Ops:
  0.0 3.6 %pre.1 = f32[8,16,2,8,128]{4,3,2,1,0:T(8,128)} custom-call(f32[2048,128]{1,0:T(8,128)} %bitcast.12, f32[2,2,32,32]{3,2,1,0:T(8,128)} %gate_hbm.1), custom_call_target="tpu_custom_call" | custom-call | tf_op jit(solution)/shard_map/pre/pallas_call | solution.py:205
  3.6 0.0 copy-start.4
  3.7 15.7 %all-to-all-start = ((f32[256,8,128]{2,1,0:T(8,128)}), f32[256,8,128]{2,1,0:T(8,128)S(1)}, u32[]{:S(2)}, u32[]{:S(2)}) async-start(f32[256,8,128]{2,1,0:T(8,128)} %bitcast.11), calls=%async_computation | async-start | bytes 2097152 | tf_op jit(solution)/shard_map/all_to_all | solution.py:224
  19.3 0.0 copy-done.4
  19.4 0.1 copy.8
  19.5 0.1 copy.9
  19.6 0.0 copy-start
  19.6 0.0 copy-start.3
  19.6 0.1 maximum_maximum_fusion.pair_ref
  19.7 0.0 copy-start.1
  19.7 0.0 copy-start.2
  19.7 0.7 copy-done
  20.3 0.0 copy-done.3
  20.3 0.0 copy-done.1
  20.4 0.0 copy-done.2
  20.4 2.3 %prep.1 = (bf16[2,256,256]{2,1,0:T(8,128)(2,1)S(1)}, bf16[2,256,256]{2,1,0:T(8,128)(2,1)S(1)}, bf16[128,256]{1,0:T(8,128)(2,1)S(1)}, bf16[128,256]{1,0:T(8,128)(2,1)S(1)}, f32[2,8,128]{2,1,0:T(8,128)S(1)}) custom-call(f32[10]{0:T(128)S(1)} %copy-done.2, s32[2,16]{1,0:T(2,128)S(1)} %bitcast.10, f32[16]{0:T(128)S(1)} %copy-done.3, ...), custom_call_target="tpu_custom_call" | custom-call | tf_op jit(solution)/shard_map/prep/pallas_call | solution.py:191
  22.7 27.5 %all-to-all-done.x_ref = f32[256,8,128]{2,1,0:T(8,128)S(1)} async-done(((f32[256,8,128]{2,1,0:T(8,128)}), f32[256,8,128]{2,1,0:T(8,128)S(1)}, u32[]{:S(2)}, u32[]{:S(2)}) %all-to-all-start) | async-done | bytes 1048608 | tf_op jit(solution)/shard_map/all_to_all | solution.py:224
  50.1 2.0 %mid.1 = f32[256,8,128]{2,1,0:T(8,128)S(1)} custom-call(f32[256,8,128]{2,1,0:T(8,128)S(1)} %all-to-all-done.x_ref, bf16[2,256,256]{2,1,0:T(8,128)(2,1)S(1)} %get-tuple-element.10.w_high, bf16[2,256,256]{2,1,0:T(8,128)(2,1)S(1)} %get-tuple-element.11.w_low, bf16[128,256]{1,0:T(8,128)(2,1)S(1)} %get-tuple-element.12.m_high, ...), custom_call_target="tpu_custom_call" | custom-call | tf_op jit(solution)/shard_map/mid/pallas_call | solution.py:225
  52.2 37.4 %all_to_all.10 = f32[256,8,128]{2,1,0:T(8,128)S(1)} all-to-all(f32[256,8,128]{2,1,0:T(8,128)S(1)} %mid.1), channel_id=1, replica_groups=mesh['grp'=16,'ing'=16] {'grp','ing'}, dimensions={0} | all-to-all | bytes 2097152 | tf_op jit(solution)/shard_map/all_to_all | solution.py:233
  89.6 1.1 %post.1 = f32[2,2,8,64,128]{4,3,2,1,0:T(8,128)} custom-call(f32[8,16,2,8,128]{4,3,2,1,0:T(8,128)S(1)} %bitcast.9), custom_call_target="tpu_custom_call" | custom-call | tf_op jit(solution)/shard_map/post/pallas_call | solution.py:234
  (2 shorter events, 0.0 us)
Async XLA Ops:
  3.6 15.7 %copy-start.4 = (f32[4,2,4,4]{3,2,1,0:T(4,128)S(1)}, f32[4,2,4,4]{3,2,1,0:T(4,128)}, u32[]{:S(2)}) copy-start(f32[4,2,4,4]{3,2,1,0:T(4,128)} %param.12) | copy-start | bytes 1540
  3.7 46.5 %all-to-all-start = ((f32[256,8,128]{2,1,0:T(8,128)}), f32[256,8,128]{2,1,0:T(8,128)S(1)}, u32[]{:S(2)}, u32[]{:S(2)}) async-start(f32[256,8,128]{2,1,0:T(8,128)} %bitcast.11), calls=%async_computation | async-start | bytes 2097152 | tf_op jit(solution)/shard_map/all_to_all | solution.py:224
  19.6 0.8 copy-start
  19.6 0.8 copy-start.3
  19.7 0.7 copy-start.1
  19.7 0.7 copy-start.2

commit v5 on v4

--- a/solution.py
+++ b/solution.py
@@ -75,8 +75,12 @@
 def pre_kernel(x_hbm, gate_hbm, out_hbm, x_ref, gate_ref, y_ref, z_ref, in_sems, out_sems):
     fetch_gates = pltpu.make_async_copy(gate_hbm, gate_ref, in_sems.at[0])
     fetch_gates.start()
-    fetch = pltpu.make_async_copy(x_hbm, x_ref, in_sems.at[1])
-    fetch.start()
+    fetches = [
+        pltpu.make_async_copy(x_hbm.at[pl.ds(1024 * c, 1024)], x_ref.at[pl.ds(1024 * c, 1024)], in_sems.at[1 + c])
+        for c in range(2)
+    ]
+    for fetch in fetches:
+        fetch.start()
     fetch_gates.wait()
     real, imag = gate_ref[0, 0], gate_ref[0, 1]
     first = split(jnp.concatenate([jnp.concatenate([real, -imag], 1), jnp.concatenate([imag, real], 1)], 0))
@@ -90,15 +94,17 @@
     ]
     second = split(jnp.concatenate([jnp.concatenate(r, 1) for r in rows], 0).T)
     first_high, first_low = first
-    stacked = jnp.concatenate([first_high, first_low, first_high], 1)
-    fetch.wait()
-    for j in range(4):
-        columns = [x_ref[pl.ds(8 * j + b, 64, stride=32), :] for b in range(8)]
-        high, rest = split(jnp.concatenate(columns, 1))
-        result = dot(stacked, jnp.concatenate([high, high, rest], 0))
-        for b in range(8):
-            at = (8 * j + b) * 64
-            y_ref[at : at + 64] = result[:, b * 128 : b * 128 + 128]
+    for c in range(2):
+        stacked = jnp.concatenate([m[:, c * 32 : c * 32 + 32] for m in (first_high, first_low, first_high)], 1)
+        fetches[c].wait()
+        for j in range(4):
+            columns = [x_ref[pl.ds(1024 * c + 8 * j + b, 32, stride=32), :] for b in range(8)]
+            high, rest = split(jnp.concatenate(columns, 1))
+            result = dot(stacked, jnp.concatenate([high, high, rest], 0))
+            for b in range(8):
+                at = (8 * j + b) * 64
+                value = result[:, b * 128 : b * 128 + 128]
+                y_ref[at : at + 64] = value if c == 0 else y_ref[at : at + 64] + value
     sub = lax.broadcasted_iota(jnp.int32, (16, 8, 128), 1)
     sends = []
     for ah in range(8):
@@ -141,18 +147,21 @@
             jnp.where(low, pltpu.roll(first, 96, 1), second),
         )
 
-    def joined(first, second, level):
-        y = dot3(split(jnp.concatenate([first, second], 1)), (w_high[level], w_low[level]))
-        return y[:, :128], y[:, 128:]
+    def join(pairs, level):
+        for start in range(0, 8, 2):
+            some = pairs[start : start + 2]
+            left = jnp.concatenate([jnp.concatenate([parts[g], parts[h]], 1) for g, h in some], 0)
+            y = dot3(split(left), (w_high[level], w_low[level]))
+            for n, (g, h) in enumerate(some):
+                rows = y[n * 128 : n * 128 + 128]
+                parts[g], parts[h] = rows[:, :128], rows[:, 128:]
 
     for g in range(0, 16, 2):
         parts[g], parts[g + 1] = trade(parts[g], parts[g + 1])
-    for g in (0, 1, 4, 5, 8, 9, 12, 13):
-        parts[g], parts[g + 2] = joined(parts[g], parts[g + 2], 0)
+    join([(g, g + 2) for g in (0, 1, 4, 5, 8, 9, 12, 13)], 0)
     for g in (0, 1, 2, 3, 8, 9, 10, 11):
         parts[g], parts[g + 4] = trade(parts[g], parts[g + 4])
-    for g in range(8):
-        parts[g], parts[g + 8] = joined(parts[g], parts[g + 8], 1)
+    join([(g, g + 8) for g in range(8)], 1)
     for g in range(0, 16, 2):
         parts[g], parts[g + 1] = trade(parts[g], parts[g + 1])
     for slot in range(16):
@@ -212,7 +221,7 @@
             pltpu.VMEM((2, 2, 32, 32), F32),
             pltpu.VMEM((2048, 128), F32),
             pltpu.VMEM((8, 16, 2, 8, 128), F32),
-            pltpu.SemaphoreType.DMA((2,)),
+            pltpu.SemaphoreType.DMA((3,)),
             pltpu.SemaphoreType.DMA((8,)),
         ],
         compiler_params=PARAMS,

time: 91 us -> 90.8 us (level)
  no operation moved by 1% of the time
where the time goes in v5:
time: 90.8 us; the launch traced here: 90.5 us
  blocking collectives  37.4 us (41%)
  waiting for transfers between devices  27.5 us (30%)
  starting transfers between devices  15.7 us (17%)
  Pallas kernels  8.91 us (10%)
  local copies, waits for them, and re-layouts  0.92 us (1%)
    all_to_all x1, blocking collectives, on_device(): back = lax.all_to_all(done, ('grp', 'ing'), 0, 0, tiled=True)  37.4 us
    all_to_all x1, waiting for transfers between devices, on_device(): lax.all_to_all(sent.reshape(256, 8, 128), ('grp', 'ing'), 0, 0, tiled=True)  27.5 us
    all_to_all x1, starting transfers between devices, on_device(): lax.all_to_all(sent.reshape(256, 8, 128), ('grp', 'ing'), 0, 0, tiled=True)  15.7 us
    pallas_call x1, Pallas kernels, on_device(): pl.pallas_call(pre_kernel, out_shape=pltpu.HBM((8, 16, 2, 8, 128), F32),...  3.54 us
    pallas_call x1, Pallas kernels, on_device(): pl.pallas_call(prep_kernel, out_shape=(jax.ShapeDtypeStruct((2, 256, 256)...  2.32 us
    pallas_call x1, Pallas kernels, on_device(): pl.pallas_call(mid_kernel, out_shape=jax.ShapeDtypeStruct((256, 8, 128),...  1.93 us
  transfers between devices with their start and end apart: 1, of which 1 were waited for; matrix products, arithmetic and copies ran while one was open for 0% of the time, Pallas kernels for 3%

profile of v5, /device:TPU:1, one launch (start us, length us, event | category | flops | bytes accessed | tf_op | source)
XLA Modules:
  0.0 90.5 jit_solution(14017103508477288428)
XLA Ops:
  0.0 3.5 %pre.1 = f32[8,16,2,8,128]{4,3,2,1,0:T(8,128)} custom-call(f32[2048,128]{1,0:T(8,128)} %bitcast.12, f32[2,2,32,32]{3,2,1,0:T(8,128)} %gate_hbm.1), custom_call_target="tpu_custom_call" | custom-call | tf_op jit(solution)/shard_map/pre/pallas_call | solution.py:214
  3.5 0.0 copy-start.4
  3.6 15.7 %all-to-all-start = ((f32[256,8,128]{2,1,0:T(8,128)}), f32[256,8,128]{2,1,0:T(8,128)S(1)}, u32[]{:S(2)}, u32[]{:S(2)}) async-start(f32[256,8,128]{2,1,0:T(8,128)} %bitcast.11), calls=%async_computation | async-start | bytes 2097152 | tf_op jit(solution)/shard_map/all_to_all | solution.py:233
  19.2 0.0 copy-done.4
  19.2 0.1 copy.8
  19.4 0.1 copy.9
  19.5 0.0 copy-start
  19.5 0.0 copy-start.3
  19.5 0.1 maximum_maximum_fusion.pair_ref
  19.6 0.0 copy-start.1
  19.6 0.0 copy-start.2
  19.6 0.7 copy-done
  20.2 0.0 copy-done.3
  20.2 0.0 copy-done.1
  20.2 0.0 copy-done.2
  20.2 2.3 %prep.1 = (bf16[2,256,256]{2,1,0:T(8,128)(2,1)S(1)}, bf16[2,256,256]{2,1,0:T(8,128)(2,1)S(1)}, bf16[128,256]{1,0:T(8,128)(2,1)S(1)}, bf16[128,256]{1,0:T(8,128)(2,1)S(1)}, f32[2,8,128]{2,1,0:T(8,128)S(1)}) custom-call(f32[10]{0:T(128)S(1)} %copy-done.2, s32[2,16]{1,0:T(2,128)S(1)} %bitcast.10, f32[16]{0:T(128)S(1)} %copy-done.3, ...), custom_call_target="tpu_custom_call" | custom-call | tf_op jit(solution)/shard_map/prep/pallas_call | solution.py:200
  22.6 27.5 %all-to-all-done.x_ref = f32[256,8,128]{2,1,0:T(8,128)S(1)} async-done(((f32[256,8,128]{2,1,0:T(8,128)}), f32[256,8,128]{2,1,0:T(8,128)S(1)}, u32[]{:S(2)}, u32[]{:S(2)}) %all-to-all-start) | async-done | bytes 1048608 | tf_op jit(solution)/shard_map/all_to_all | solution.py:233
  50.0 1.9 %mid.1 = f32[256,8,128]{2,1,0:T(8,128)S(1)} custom-call(f32[256,8,128]{2,1,0:T(8,128)S(1)} %all-to-all-done.x_ref, bf16[2,256,256]{2,1,0:T(8,128)(2,1)S(1)} %get-tuple-element.10.w_high, bf16[2,256,256]{2,1,0:T(8,128)(2,1)S(1)} %get-tuple-element.11.w_low, bf16[128,256]{1,0:T(8,128)(2,1)S(1)} %get-tuple-element.12.m_high, ...), custom_call_target="tpu_custom_call" | custom-call | tf_op jit(solution)/shard_map/mid/pallas_call | solution.py:234
  52.0 37.4 %all_to_all.10 = f32[256,8,128]{2,1,0:T(8,128)S(1)} all-to-all(f32[256,8,128]{2,1,0:T(8,128)S(1)} %mid.1), channel_id=1, replica_groups=mesh['grp'=16,'ing'=16] {'grp','ing'}, dimensions={0} | all-to-all | bytes 2097152 | tf_op jit(solution)/shard_map/all_to_all | solution.py:242
  89.4 1.1 %post.1 = f32[2,2,8,64,128]{4,3,2,1,0:T(8,128)} custom-call(f32[8,16,2,8,128]{4,3,2,1,0:T(8,128)S(1)} %bitcast.9), custom_call_target="tpu_custom_call" | custom-call | tf_op jit(solution)/shard_map/post/pallas_call | solution.py:243
  (2 shorter events, 0.0 us)
Async XLA Ops:
  3.5 15.7 %copy-start.4 = (f32[4,2,4,4]{3,2,1,0:T(4,128)S(1)}, f32[4,2,4,4]{3,2,1,0:T(4,128)}, u32[]{:S(2)}) copy-start(f32[4,2,4,4]{3,2,1,0:T(4,128)} %param.12) | copy-start | bytes 1540
  3.6 46.5 %all-to-all-start = ((f32[256,8,128]{2,1,0:T(8,128)}), f32[256,8,128]{2,1,0:T(8,128)S(1)}, u32[]{:S(2)}, u32[]{:S(2)}) async-start(f32[256,8,128]{2,1,0:T(8,128)} %bitcast.11), calls=%async_computation | async-start | bytes 2097152 | tf_op jit(solution)/shard_map/all_to_all | solution.py:233
  19.5 0.8 copy-start
  19.5 0.8 copy-start.3
  19.6 0.7 copy-start.1
  19.6 0.7 copy-start.2

commit v6 on v5

--- a/solution.py
+++ b/solution.py
@@ -180,9 +180,9 @@
             turned = z.T
             for c in range(2):
                 z_ref[c, top, ah] = turned[c * 64 : c * 64 + 64]
-        send = pltpu.make_async_copy(z_ref.at[:, :, ah], out_hbm.at[:, :, ah], sems.at[ah])
-        send.start()
-        sends.append(send)
+            send = pltpu.make_async_copy(z_ref.at[:, top, ah], out_hbm.at[:, top, ah], sems.at[2 * ah + top])
+            send.start()
+            sends.append(send)
     for send in sends:
         send.wait()
 
@@ -245,7 +245,7 @@
         out_shape=pltpu.HBM((2, 2, 8, 64, 128), F32),
         in_specs=[VMEM],
         out_specs=HBM,
-        scratch_shapes=[pltpu.VMEM((2, 2, 8, 64, 128), F32), pltpu.SemaphoreType.DMA((8,))],
+        scratch_shapes=[pltpu.VMEM((2, 2, 8, 64, 128), F32), pltpu.SemaphoreType.DMA((16,))],
         compiler_params=PARAMS,
         name="post",
     )(back.reshape(8, 16, 2, 8, 128))

time: 90.8 us -> 90.8 us (level)
  no operation moved by 1% of the time
where the time goes in v6:
time: 90.8 us; the launch traced here: 90.6 us
  blocking collectives  37.4 us (41%)
  waiting for transfers between devices  27.5 us (30%)
  starting transfers between devices  15.7 us (17%)
  Pallas kernels  8.98 us (10%)
  local copies, waits for them, and re-layouts  0.92 us (1%)
    all_to_all x1, blocking collectives, on_device(): back = lax.all_to_all(done, ('grp', 'ing'), 0, 0, tiled=True)  37.4 us
    all_to_all x1, waiting for transfers between devices, on_device(): lax.all_to_all(sent.reshape(256, 8, 128), ('grp', 'ing'), 0, 0, tiled=True)  27.5 us
    all_to_all x1, starting transfers between devices, on_device(): lax.all_to_all(sent.reshape(256, 8, 128), ('grp', 'ing'), 0, 0, tiled=True)  15.7 us
    pallas_call x1, Pallas kernels, on_device(): pl.pallas_call(pre_kernel, out_shape=pltpu.HBM((8, 16, 2, 8, 128), F32),...  3.54 us
    pallas_call x1, Pallas kernels, on_device(): pl.pallas_call(prep_kernel, out_shape=(jax.ShapeDtypeStruct((2, 256, 256)...  2.32 us
    pallas_call x1, Pallas kernels, on_device(): pl.pallas_call(mid_kernel, out_shape=jax.ShapeDtypeStruct((256, 8, 128),...  1.93 us
  transfers between devices with their start and end apart: 1, of which 1 were waited for; matrix products, arithmetic and copies ran while one was open for 0% of the time, Pallas kernels for 3%

profile of v6, /device:TPU:1, one launch (start us, length us, event | category | flops | bytes accessed | tf_op | source)
XLA Modules:
  0.0 90.6 jit_solution(2718441875785361795)
XLA Ops:
  0.0 3.5 %pre.1 = f32[8,16,2,8,128]{4,3,2,1,0:T(8,128)} custom-call(f32[2048,128]{1,0:T(8,128)} %bitcast.12, f32[2,2,32,32]{3,2,1,0:T(8,128)} %gate_hbm.1), custom_call_target="tpu_custom_call" | custom-call | tf_op jit(solution)/shard_map/pre/pallas_call | solution.py:214
  3.5 0.0 copy-start.4
  3.6 15.7 %all-to-all-start = ((f32[256,8,128]{2,1,0:T(8,128)}), f32[256,8,128]{2,1,0:T(8,128)S(1)}, u32[]{:S(2)}, u32[]{:S(2)}) async-start(f32[256,8,128]{2,1,0:T(8,128)} %bitcast.11), calls=%async_computation | async-start | bytes 2097152 | tf_op jit(solution)/shard_map/all_to_all | solution.py:233
  19.2 0.0 copy-done.4
  19.2 0.1 copy.8
  19.4 0.1 copy.9
  19.5 0.0 copy-start
  19.5 0.0 copy-start.3
  19.5 0.1 maximum_maximum_fusion.pair_ref
  19.6 0.0 copy-start.1
  19.6 0.0 copy-start.2
  19.6 0.7 copy-done
  20.2 0.0 copy-done.3
  20.2 0.0 copy-done.1
  20.2 0.0 copy-done.2
  20.2 2.3 %prep.1 = (bf16[2,256,256]{2,1,0:T(8,128)(2,1)S(1)}, bf16[2,256,256]{2,1,0:T(8,128)(2,1)S(1)}, bf16[128,256]{1,0:T(8,128)(2,1)S(1)}, bf16[128,256]{1,0:T(8,128)(2,1)S(1)}, f32[2,8,128]{2,1,0:T(8,128)S(1)}) custom-call(f32[10]{0:T(128)S(1)} %copy-done.2, s32[2,16]{1,0:T(2,128)S(1)} %bitcast.10, f32[16]{0:T(128)S(1)} %copy-done.3, ...), custom_call_target="tpu_custom_call" | custom-call | tf_op jit(solution)/shard_map/prep/pallas_call | solution.py:200
  22.6 27.5 %all-to-all-done.x_ref = f32[256,8,128]{2,1,0:T(8,128)S(1)} async-done(((f32[256,8,128]{2,1,0:T(8,128)}), f32[256,8,128]{2,1,0:T(8,128)S(1)}, u32[]{:S(2)}, u32[]{:S(2)}) %all-to-all-start) | async-done | bytes 1048608 | tf_op jit(solution)/shard_map/all_to_all | solution.py:233
  50.0 1.9 %mid.1 = f32[256,8,128]{2,1,0:T(8,128)S(1)} custom-call(f32[256,8,128]{2,1,0:T(8,128)S(1)} %all-to-all-done.x_ref, bf16[2,256,256]{2,1,0:T(8,128)(2,1)S(1)} %get-tuple-element.10.w_high, bf16[2,256,256]{2,1,0:T(8,128)(2,1)S(1)} %get-tuple-element.11.w_low, bf16[128,256]{1,0:T(8,128)(2,1)S(1)} %get-tuple-element.12.m_high, ...), custom_call_target="tpu_custom_call" | custom-call | tf_op jit(solution)/shard_map/mid/pallas_call | solution.py:234
  52.0 37.4 %all_to_all.10 = f32[256,8,128]{2,1,0:T(8,128)S(1)} all-to-all(f32[256,8,128]{2,1,0:T(8,128)S(1)} %mid.1), channel_id=1, replica_groups=mesh['grp'=16,'ing'=16] {'grp','ing'}, dimensions={0} | all-to-all | bytes 2097152 | tf_op jit(solution)/shard_map/all_to_all | solution.py:242
  89.4 1.2 %post.1 = f32[2,2,8,64,128]{4,3,2,1,0:T(8,128)} custom-call(f32[8,16,2,8,128]{4,3,2,1,0:T(8,128)S(1)} %bitcast.9), custom_call_target="tpu_custom_call" | custom-call | tf_op jit(solution)/shard_map/post/pallas_call | solution.py:243
  (2 shorter events, 0.0 us)
Async XLA Ops:
  3.5 15.7 %copy-start.4 = (f32[4,2,4,4]{3,2,1,0:T(4,128)S(1)}, f32[4,2,4,4]{3,2,1,0:T(4,128)}, u32[]{:S(2)}) copy-start(f32[4,2,4,4]{3,2,1,0:T(4,128)} %param.12) | copy-start | bytes 1540
  3.6 46.5 %all-to-all-start = ((f32[256,8,128]{2,1,0:T(8,128)}), f32[256,8,128]{2,1,0:T(8,128)S(1)}, u32[]{:S(2)}, u32[]{:S(2)}) async-start(f32[256,8,128]{2,1,0:T(8,128)} %bitcast.11), calls=%async_computation | async-start | bytes 2097152 | tf_op jit(solution)/shard_map/all_to_all | solution.py:233
  19.5 0.8 copy-start
  19.5 0.8 copy-start.3
  19.6 0.7 copy-start.1
  19.6 0.7 copy-start.2

commit v7 on v6

--- a/solution.py
+++ b/solution.py
@@ -84,17 +84,18 @@
     fetch_gates.wait()
     real, imag = gate_ref[0, 0], gate_ref[0, 1]
     first = split(jnp.concatenate([jnp.concatenate([real, -imag], 1), jnp.concatenate([imag, real], 1)], 0))
-    real, imag = gate_ref[1, 0], gate_ref[1, 1]
-    zero = jnp.zeros_like(real)
-    rows = [
-        [real, zero, -imag, zero],
-        [zero, real, zero, -imag],
-        [imag, zero, real, zero],
-        [zero, imag, zero, real],
-    ]
-    second = split(jnp.concatenate([jnp.concatenate(r, 1) for r in rows], 0).T)
     first_high, first_low = first
     for c in range(2):
+        if c == 1:
+            real, imag = gate_ref[1, 0], gate_ref[1, 1]
+            zero = jnp.zeros_like(real)
+            rows = [
+                [real, zero, -imag, zero],
+                [zero, real, zero, -imag],
+                [imag, zero, real, zero],
+                [zero, imag, zero, real],
+            ]
+            second = split(jnp.concatenate([jnp.concatenate(r, 1) for r in rows], 0).T)
         stacked = jnp.concatenate([m[:, c * 32 : c * 32 + 32] for m in (first_high, first_low, first_high)], 1)
         fetches[c].wait()
         for j in range(4):

time: 90.8 us -> 90.9 us (level)
  no operation moved by 1% of the time
where the time goes in v7:
time: 90.9 us; the launch traced here: 90.6 us
  blocking collectives  37.4 us (41%)
  waiting for transfers between devices  27.5 us (30%)
  starting transfers between devices  15.7 us (17%)
  Pallas kernels  8.98 us (10%)
  local copies, waits for them, and re-layouts  0.92 us (1%)
    all_to_all x1, blocking collectives, on_device(): back = lax.all_to_all(done, ('grp', 'ing'), 0, 0, tiled=True)  37.4 us
    all_to_all x1, waiting for transfers between devices, on_device(): lax.all_to_all(sent.reshape(256, 8, 128), ('grp', 'ing'), 0, 0, tiled=True)  27.5 us
    all_to_all x1, starting transfers between devices, on_device(): lax.all_to_all(sent.reshape(256, 8, 128), ('grp', 'ing'), 0, 0, tiled=True)  15.7 us
    pallas_call x1, Pallas kernels, on_device(): pl.pallas_call(pre_kernel, out_shape=pltpu.HBM((8, 16, 2, 8, 128), F32),...  3.54 us
    pallas_call x1, Pallas kernels, on_device(): pl.pallas_call(prep_kernel, out_shape=(jax.ShapeDtypeStruct((2, 256, 256)...  2.32 us
    pallas_call x1, Pallas kernels, on_device(): pl.pallas_call(mid_kernel, out_shape=jax.ShapeDtypeStruct((256, 8, 128),...  1.93 us
  transfers between devices with their start and end apart: 1, of which 1 were waited for; matrix products, arithmetic and copies ran while one was open for 0% of the time, Pallas kernels for 3%

profile of v7, /device:TPU:1, one launch (start us, length us, event | category | flops | bytes accessed | tf_op | source)
XLA Modules:
  0.0 90.6 jit_solution(16682768579125709839)
XLA Ops:
  0.0 3.5 %pre.1 = f32[8,16,2,8,128]{4,3,2,1,0:T(8,128)} custom-call(f32[2048,128]{1,0:T(8,128)} %bitcast.12, f32[2,2,32,32]{3,2,1,0:T(8,128)} %gate_hbm.1), custom_call_target="tpu_custom_call" | custom-call | tf_op jit(solution)/shard_map/pre/pallas_call | solution.py:215
  3.6 0.0 copy-start.4
  3.6 15.7 %all-to-all-start = ((f32[256,8,128]{2,1,0:T(8,128)}), f32[256,8,128]{2,1,0:T(8,128)S(1)}, u32[]{:S(2)}, u32[]{:S(2)}) async-start(f32[256,8,128]{2,1,0:T(8,128)} %bitcast.11), calls=%async_computation | async-start | bytes 2097152 | tf_op jit(solution)/shard_map/all_to_all | solution.py:234
  19.2 0.0 copy-done.4
  19.3 0.1 copy.8
  19.4 0.1 copy.9
  19.5 0.0 copy-start
  19.5 0.0 copy-start.3
  19.5 0.1 maximum_maximum_fusion.pair_ref
  19.6 0.0 copy-start.1
  19.6 0.0 copy-start.2
  19.6 0.7 copy-done
  20.2 0.0 copy-done.3
  20.2 0.0 copy-done.1
  20.3 0.0 copy-done.2
  20.3 2.3 %prep.1 = (bf16[2,256,256]{2,1,0:T(8,128)(2,1)S(1)}, bf16[2,256,256]{2,1,0:T(8,128)(2,1)S(1)}, bf16[128,256]{1,0:T(8,128)(2,1)S(1)}, bf16[128,256]{1,0:T(8,128)(2,1)S(1)}, f32[2,8,128]{2,1,0:T(8,128)S(1)}) custom-call(f32[10]{0:T(128)S(1)} %copy-done.2, s32[2,16]{1,0:T(2,128)S(1)} %bitcast.10, f32[16]{0:T(128)S(1)} %copy-done.3, ...), custom_call_target="tpu_custom_call" | custom-call | tf_op jit(solution)/shard_map/prep/pallas_call | solution.py:201
  22.6 27.5 %all-to-all-done.x_ref = f32[256,8,128]{2,1,0:T(8,128)S(1)} async-done(((f32[256,8,128]{2,1,0:T(8,128)}), f32[256,8,128]{2,1,0:T(8,128)S(1)}, u32[]{:S(2)}, u32[]{:S(2)}) %all-to-all-start) | async-done | bytes 1048608 | tf_op jit(solution)/shard_map/all_to_all | solution.py:234
  50.0 1.9 %mid.1 = f32[256,8,128]{2,1,0:T(8,128)S(1)} custom-call(f32[256,8,128]{2,1,0:T(8,128)S(1)} %all-to-all-done.x_ref, bf16[2,256,256]{2,1,0:T(8,128)(2,1)S(1)} %get-tuple-element.10.w_high, bf16[2,256,256]{2,1,0:T(8,128)(2,1)S(1)} %get-tuple-element.11.w_low, bf16[128,256]{1,0:T(8,128)(2,1)S(1)} %get-tuple-element.12.m_high, ...), custom_call_target="tpu_custom_call" | custom-call | tf_op jit(solution)/shard_map/mid/pallas_call | solution.py:235
  52.0 37.4 %all_to_all.10 = f32[256,8,128]{2,1,0:T(8,128)S(1)} all-to-all(f32[256,8,128]{2,1,0:T(8,128)S(1)} %mid.1), channel_id=1, replica_groups=mesh['grp'=16,'ing'=16] {'grp','ing'}, dimensions={0} | all-to-all | bytes 2097152 | tf_op jit(solution)/shard_map/all_to_all | solution.py:243
  89.4 1.2 %post.1 = f32[2,2,8,64,128]{4,3,2,1,0:T(8,128)} custom-call(f32[8,16,2,8,128]{4,3,2,1,0:T(8,128)S(1)} %bitcast.9), custom_call_target="tpu_custom_call" | custom-call | tf_op jit(solution)/shard_map/post/pallas_call | solution.py:244
  (2 shorter events, 0.0 us)
Async XLA Ops:
  3.6 15.7 %copy-start.4 = (f32[4,2,4,4]{3,2,1,0:T(4,128)S(1)}, f32[4,2,4,4]{3,2,1,0:T(4,128)}, u32[]{:S(2)}) copy-start(f32[4,2,4,4]{3,2,1,0:T(4,128)} %param.12) | copy-start | bytes 1540
  3.6 46.5 %all-to-all-start = ((f32[256,8,128]{2,1,0:T(8,128)}), f32[256,8,128]{2,1,0:T(8,128)S(1)}, u32[]{:S(2)}, u32[]{:S(2)}) async-start(f32[256,8,128]{2,1,0:T(8,128)} %bitcast.11), calls=%async_computation | async-start | bytes 2097152 | tf_op jit(solution)/shard_map/all_to_all | solution.py:234
  19.5 0.8 copy-start
  19.5 0.8 copy-start.3
  19.6 0.7 copy-start.1
  19.6 0.7 copy-start.2
